TPU v7x, 32 devices: a whole 2x2x4 slice. The times are simulated.
32 devices in a mesh: ctx: 8 (over z, x), head: 4 (over y, core).
Axes of the slice: x: 2, y: 2, z: 4, core: 2. Of those that a mesh axis runs over, the one named last changes fastest.
Arguments:
- channels_in: bfloat16 [12288, 8192], P('ctx', 'head'), may hold values from -6 to 6
- state_maps: bfloat16 [12288, 2, 1024], P('ctx', None, 'head'), may hold values from -6 to 6
- gate_in: bfloat16 [12288, 8192], P('ctx', 'head'), may hold values from -6 to 6
- step_raw: float32 [12288, 128], P('ctx', 'head'), may hold values from -1.2 to 80
- convolution_channel_taps: float32 [4, 8192], P(None, 'head'), may hold values from -3 to 3
- conv_maps: float32 [4, 2, 1024], P(None, None, 'head'), may hold values from -3 to 3
- head_rates: float32 [2, 128], P(None, 'head'), may hold values from -8 to 0
- skip_gain: float32 [128], P('head'), may hold values from 0.5 to 2
- norm_gain: float32 [8192], P('head'), may hold values from 0.5 to 1.5
Outputs:
- relaid: bfloat16 [12288, 8192], P(('ctx', 'head'))
All inputs are finite; a program needn't handle non-finite values.
Results may differ from a plain program's by a relative error of at most 0.006.
Values may be sent and summed in bfloat16 or wider, within the bound.
No kernel may reach another device: no remote copies, remote signals or barrier semaphores. Data moves between devices by JAX's collectives and lax.ppermute only.
A program may use at most 192 MiB of HBM per device.

v0:
```python
import jax
import jax.numpy as jnp
from jax import lax
from jax.sharding import PartitionSpec as P

HEAD_DIM = 64
STATE = 128
TAPS = 4
STRETCH = 256


HIGHEST_PRECISION = lax.Precision.HIGHEST
EPSILON = 1e-05


def passed_along(value, axis, by):
    peers = lax.axis_size(axis)
    pairs = [(i, i + by) for i in range(peers) if 0 <= i + by < peers]
    return lax.ppermute(value, axis, pairs)


def entering_2(part, axis, combine, identity):
    place = lax.axis_index(axis)
    gathered = jax.tree.map(lambda a: lax.all_gather(a, axis), part)
    state = jax.tree.map(lambda a, e: jnp.zeros_like(a) + jnp.asarray(e, a.dtype), part, identity)

    def one(hop, state):
        return combine(
            state, jax.tree.map(lambda a: lax.dynamic_index_in_dim(a, hop, 0, False), gathered)
        )

    return lax.fori_loop(0, place, one, state)


def stretch_terms(pieces):
    values, b_maps, c_maps, step_sizes, log_rates = pieces
    length = values.shape[0]
    cumlog = jnp.cumsum(log_rates, axis=0)
    causal = jnp.arange(length)[:, None] >= jnp.arange(length)[None, :]
    log_gaps = cumlog[:, None] - cumlog[None, :]
    decays = jnp.exp(jnp.where(causal[:, :, None, None], log_gaps, -jnp.inf))
    scores = jnp.einsum("tgn,sgn->tsg", c_maps, b_maps, preferred_element_type=jnp.float32)
    weights = (scores[..., None] * decays * step_sizes[None]).astype(jnp.bfloat16)
    inside = jnp.einsum("tsgh,sghp->tghp", weights, values, preferred_element_type=jnp.float32)
    tail_weights = jnp.exp(cumlog[-1][None] - cumlog) * step_sizes
    tail = (tail_weights[..., None] * values.astype(jnp.float32)).astype(jnp.bfloat16)
    summary = jnp.einsum("sghp,sgn->ghpn", tail, b_maps, preferred_element_type=jnp.float32)
    return (inside, summary, cumlog)


def combine(earlier, later):
    return (earlier[0] + later[0], jnp.exp(later[0])[..., None, None] * earlier[1] + later[1])


def per_device(
    channels_in,
    state_maps,
    gate_in,
    step_raw,
    convolution_channel_taps,
    conv_maps,
    head_rates,
    skip_gain,
    norm_gain,
):
    count_of_rows, channel_count = channels_in.shape
    head_count = step_raw.shape[1]
    map_width = state_maps.shape[2]
    groups = map_width // STATE
    per_group = head_count // groups
    current = jnp.concatenate([channels_in, state_maps.reshape(count_of_rows, 2 * map_width)], 1)
    previous = passed_along(current[count_of_rows - (TAPS - 1) :], "ctx", 1)
    padded = jnp.concatenate([previous, current], 0).astype(jnp.float32)
    kernel = jnp.concatenate([convolution_channel_taps, conv_maps.reshape(TAPS, 2 * map_width)], 1)
    summed = jnp.zeros((count_of_rows, channel_count + 2 * map_width), jnp.float32)
    for offset in range(TAPS):
        summed = summed + kernel[offset] * padded[offset : offset + count_of_rows]
    conved = jax.nn.silu(summed).astype(jnp.bfloat16)
    stretch_count = count_of_rows // STRETCH
    values = conved[:, :channel_count].reshape(stretch_count, STRETCH, groups, per_group, HEAD_DIM)
    b_maps = conved[:, channel_count : channel_count + map_width].reshape(
        stretch_count, STRETCH, groups, STATE
    )
    c_maps = conved[:, channel_count + map_width :].reshape(stretch_count, STRETCH, groups, STATE)
    step_sizes = jax.nn.softplus(step_raw + head_rates[0][None, :])
    log_rates = -jnp.exp(head_rates[1])[None, :] * step_sizes
    step_sizes = step_sizes.reshape(stretch_count, STRETCH, groups, per_group)
    log_rates = log_rates.reshape(stretch_count, STRETCH, groups, per_group)
    inside, summary, cumlog = lax.map(
        stretch_terms, (values, b_maps, c_maps, step_sizes, log_rates)
    )
    final_logs = cumlog[:, -1]

    def advance(carried, pieces):
        final_log, summary_term = pieces
        return (jnp.exp(final_log)[..., None, None] * carried + summary_term, carried)

    initial = jnp.zeros(summary.shape[1:], jnp.float32)
    dev_state, enter_local = lax.scan(advance, initial, (final_logs, summary))
    dev_log = jnp.sum(final_logs, axis=0)
    identity = (jnp.zeros_like(dev_log), jnp.zeros_like(dev_state))
    scanned = entering_2((dev_log, dev_state), "ctx", combine, identity)
    incoming = scanned[1]
    before_logs = jnp.cumsum(final_logs, axis=0) - final_logs
    entering = jnp.exp(before_logs)[..., None, None] * incoming[None] + enter_local
    c_wide = c_maps.astype(jnp.float32)
    from_state = (
        jnp.einsum("ctgn,cghpn->ctghp", c_wide, entering, precision=HIGHEST_PRECISION)
        * jnp.exp(cumlog)[..., None]
    )
    skipped = skip_gain.reshape(groups, per_group)[..., None] * values.astype(jnp.float32)
    ssm_out = (inside + from_state + skipped).reshape(count_of_rows, groups, per_group * HEAD_DIM)
    gating = jax.nn.silu(gate_in.astype(jnp.float32)).reshape(
        count_of_rows, groups, per_group * HEAD_DIM
    )
    gated_out = ssm_out * gating
    inverse_rms = lax.rsqrt(jnp.mean(gated_out * gated_out, axis=-1, keepdims=True) + EPSILON)
    normed = gated_out * inverse_rms * norm_gain.reshape(groups, per_group * HEAD_DIM)
    normed = normed.reshape(count_of_rows, channel_count).astype(jnp.bfloat16)
    return lax.all_to_all(normed, "head", split_axis=0, concat_axis=1, tiled=True)


def solution(mesh):
    return jax.shard_map(
        per_device,
        mesh=mesh,
        in_specs=(
            P("ctx", "head"),
            P("ctx", None, "head"),
            P("ctx", "head"),
            P("ctx", "head"),
            P(None, "head"),
            P(None, None, "head"),
            P(None, "head"),
            P("head"),
            P("head"),
        ),
        out_specs=P(("ctx", "head"), None),
        check_vma=False,
    )
```

profile of v0, /device:TPU:26, one launch (start us, length us, event | category | flops | bytes accessed | tf_op | source)
XLA Modules:
  0.0 483.0 jit_solution(17739087428586697370)
XLA Ops:
  6.6 3.6 constant_dynamic-update-slice_fusion.3
  10.7 3.1 copy-done.1
  13.8 1.3 collective-permute-start
  17.0 2.5 collective-permute-done
  19.5 11.1 %maximum_convert_fusion = f32[1539,2560]{1,0:T(8,128)} fusion(bf16[1536,2560]{1,0:T(8,128)(2,1)} %copy-done.1, bf16[3,2560]{1,0:T(4,128)(2,1)S(1)} %collective-permute-done), kind=kLoop, calls=%fused_computation.67 | loop fusion | flops 15759360 | bytes 23639040 | tf_op jit(solution)/shard_map/convert_element_type | solution.py:73
  30.5 22.1 %multiply_convert_fusion.6 = bf16[1536,2560]{1,0:T(8,128)(2,1)S(1)} fusion(f32[1539,2560]{1,0:T(8,128)} %maximum_convert_fusion, f32[2560]{0:T(1024)S(1)} %get-tuple-element.187, f32[2560]{0:T(1024)S(1)} %get-tuple-element.188, f32[2560]{0:T(1024)S(1)} %get-tuple-element.189, f32[2560]{0:T(1024)S(1)} %get-tuple-element.186), kind=kLoop, calls=%fused_computation.54 | loop fusion | flops 47185920 | bytes 70819840 | tf_op jit(solution)/shard_map/convert_element_type | solution.py:78
  53.6 3.5 slice.81
  57.1 2.0 reshape.113
  59.2 18.6 %reshape.125 = bf16[6,256,2,16,64]{4,3,2,1,0:T(8,128)(2,1)} reshape(bf16[1536,2048]{1,0:T(8,128)(2,1)} %slice.81) | data formatting | bytes 12582912 | tf_op jit(solution)/shard_map/reshape | solution.py:80
  77.8 14.8 %copy.61 = bf16[6,256,2,16,64]{1,4,3,2,0:T(8,128)(2,1)} copy(bf16[6,256,2,16,64]{4,3,2,1,0:T(8,128)(2,1)} %reshape.125) | data formatting | bytes 12582912 | tf_op jit(solution)/shard_map/while | solution.py:89
  93.7 3.5 broadcast.43.clone
  97.2 69.7 %while.39 = (s32[]{:T(128)}, f32[6,256,2,16,64]{1,4,3,2,0:T(8,128)}, f32[6,2,16,64,128]{4,3,2,1,0:T(8,128)}, f32[6,256,2,16]{1,3,2,0:T(8,128)S(1)}, bf16[6,256,2...) while((s32[]{:T(128)}, ...), condition=%wide.region_3.4_spmd, body=%wide.region_0.3_spmd.sunk | while | flops 449413216 | bytes 9084545 | solution.py:89
  98.3 1.2 reduce-window.12
  99.8 1.1 constant_dynamic-slice_fusion.7
  101.4 4.5 bitcast_dynamic-update-slice_fusion.4
  106.1 2.6 fusion.51
  110.0 1.2 reduce-window.12
  111.4 1.1 constant_dynamic-slice_fusion.7
  113.0 4.5 bitcast_dynamic-update-slice_fusion.4
  117.8 2.6 fusion.51
  121.6 1.2 reduce-window.12
  123.1 1.1 constant_dynamic-slice_fusion.7
  124.6 4.5 bitcast_dynamic-update-slice_fusion.4
  129.4 2.6 fusion.51
  133.2 1.2 reduce-window.12
  134.7 1.1 constant_dynamic-slice_fusion.7
  136.3 4.5 bitcast_dynamic-update-slice_fusion.4
  141.0 2.6 fusion.51
  144.8 1.2 reduce-window.12
  147.9 4.5 bitcast_dynamic-update-slice_fusion.4
  152.6 2.6 fusion.51
  156.4 1.2 reduce-window.12
  157.9 1.1 constant_dynamic-slice_fusion.7
  159.5 4.5 bitcast_dynamic-update-slice_fusion.4
  164.2 2.6 fusion.51
  166.9 2.1 copy.66
  169.7 3.4 broadcast.43
  173.1 15.0 %while.41 = (s32[]{:T(128)}, f32[2,16,64,128]{3,2,1,0:T(8,128)S(1)}, f32[6,2,16,64,128]{4,3,2,1,0:T(8,128)}, f32[6,2,16]{2,1,0:T(2,128)S(1)}, f32[6,2,16,64,128]{4,3,2,1,0:T(8,128)}, /*index=5*/s32[]{:T(128)}, s32[]{:T(128)}) while((s32[]{:T(128)}, f32[2,16,64,128]{3,2,1,0:T(8,128)S(1)}, f32[6,2,16,64,128]{4,3,2,1,0:T(8,128)}, ...), condition=%wide.region_7.8_spmd.clone, body=%wide.region_6.7_spmd.clone.sunk | while | flops 1048579 | bytes 5243872 | solution.py:99
  174.2 1.4 bitcast_add_fusion.5
  176.7 1.4 bitcast_add_fusion.5
  179.2 1.4 bitcast_add_fusion.5
  180.6 1.1 bitcast_dynamic-update-slice_fusion.5
  181.7 1.4 bitcast_add_fusion.5
  184.2 1.4 bitcast_add_fusion.5
  186.7 1.4 bitcast_add_fusion.5
  189.2 8.6 %copy.70 = bf16[1536,2048]{0,1:T(8,128)(2,1)} copy(bf16[1536,2048]{1,0:T(8,128)(2,1)} %param.17) | data formatting | bytes 12582912 | tf_op args[2]
  197.8 9.3 %convert_multiply_fusion = f32[1536,2048]{0,1:T(8,128)} fusion(bf16[1536,2048]{0,1:T(8,128)(2,1)} %copy.70), kind=kLoop, calls=%fused_computation.52 | loop fusion | flops 15728640 | bytes 18874368 | tf_op jit(solution)/shard_map/jit(silu)/mul | solution.py:113
  207.1 16.0 %reshape.117 = f32[6,256,2,16,64]{1,0,4,3,2:T(8,128)} reshape(f32[1536,2048]{0,1:T(8,128)} %convert_multiply_fusion) | data formatting | bytes 25165824 | tf_op jit(solution)/shard_map/reshape | solution.py:113
  223.2 16.5 %all-gather.2 = f32[8,2,16]{2,1,0:T(2,128)S(1)} all-gather(f32[1,2,16]{2,1,0:T(2,128)S(1)} %bitcast.186), channel_id=2, replica_groups=mesh['ctx'=8,'head'=4] {'ctx'}, dimensions={0}, use_global_device_ids=true | all-gather | bytes 1152 | tf_op jit(solution)/shard_map/all_gather | solution.py:24
  240.5 71.4 %all-gather.5.cloned.1.call-done = f32[16,16,64,128]{3,2,1,0:T(8,128)} async-done(((f32[2,16,64,128]{3,2,1,0:T(8,128)}), f32[16,16,64,128]{3,2,1,0:T(8,128)}) %all-gather.5.cloned.1.call-update) | async-done | bytes 8388624 | tf_op jit(solution)/shard_map/all_gather | solution.py:24
  312.0 10.7 %while.40 = (s32[]{:T(128)}, f32[2,16,64,128]{3,2,1,0:T(8,128)S(1)}, s32[]{:T(128)}, f32[8,2,16]{2,1,0:T(2,128)S(1)}, f32[8,2,16,64,128]{4,3,2,1,0:T(8,128)}, /*index=5*/s32[]{:T(128)}, s32[]{:T(128)}, s32[]{:T(128)}) while((s32[]{:T(128)}, f32[2,16,64,128]{3,2,1,0:T(8,128)S(1)}, s32[]{:T(128)}, f32[8,2,16]{2,1,0:T(2,128)S(1)}, ...), condition=%wide.region_9.10_spmd, body=%wide.region_8.9_spmd.sunk | while | flops 524293 | bytes 3146239 | solution.py:32
  312.1 1.4 bitcast_add_fusion.4
  313.6 1.4 bitcast_add_fusion.4
  315.1 1.4 bitcast_add_fusion.4
  316.6 1.4 bitcast_add_fusion.4
  318.1 1.4 bitcast_add_fusion.4
  319.6 1.4 bitcast_add_fusion.4
  321.1 1.4 bitcast_add_fusion.4
  322.8 21.7 %fusion.32 = (f32[6,256,2]{1,2,0:T(2,128)S(1)}, f32[6,256,2,16,64]{1,4,3,2,0:T(8,128)}) fusion(f32[6,256,2,16,64]{1,0,4,3,2:T(8,128)} %reshape.117, bf16[6,256,2,16,64]{1,4,3,2,0:T(8,128)(2,1)} %get-tuple-element.449, f32[2,16]{1,0:T(2,128)S(1)} %mul.190, f32[6,256,2,16,64]{1,4,3,2,0:T(8,128)} %get-tuple-element.126, f32[6,256,2,16]{1,3,2,0:T(8,128)S(1)} %exp.57, ...), kind=kOutput, calls=%fused_computation.66 | convolution fusion | flops 4860146688 | bytes 52376448 | tf_op jit(solution)/shard_map/ctgn,cghpn->ctghp/dot_general | solution.py:108
  344.5 21.7 %copy.69 = f32[6,256,2,16,64]{1,0,4,3,2:T(8,128)} copy(f32[6,256,2,16,64]{1,4,3,2,0:T(8,128)} %get-tuple-element.241) | data formatting | bytes 25165824 | tf_op jit(solution)/shard_map/add | solution.py:112
  366.2 17.1 %copy.89 = f32[256,8,6,256]{3,1,2,0:T(8,128)} copy(f32[256,8,6,256]{3,2,1,0:T(8,128)} %bitcast.172) | data formatting | bytes 25165824
  383.3 9.2 %fusion.28 = bf16[1536,2048]{0,1:T(8,128)(2,1)S(1)} fusion(f32[1536,2048]{0,1:T(8,128)} %bitcast.173, f32[2048]{0:T(1024)S(1)} %copy-done.5, f32[1536,2]{0,1:T(2,128)S(1)} %bitcast.183, bf16[1536,2048]{0,1:T(8,128)(2,1)} %copy.70), kind=kLoop, calls=%fused_computation.60 | loop fusion | flops 28311552 | bytes 25186304 | tf_op jit(solution)/shard_map/convert_element_type | solution.py:119
  393.2 74.2 %all_to_all.19 = bf16[4,384,2048]{1,2,0:T(8,128)(2,1)} all-to-all(bf16[4,384,2048]{1,2,0:T(8,128)(2,1)S(1)} %bitcast.174), channel_id=1, replica_groups=mesh['ctx'=8,'head'=4] {'head'}, dimensions={0} | all-to-all | bytes 12582912 | tf_op jit(solution)/shard_map/all_to_all | solution.py:120
  467.4 8.6 %copy.73 = bf16[384,8192]{1,0:T(8,128)(2,1)} copy(bf16[384,8192]{0,1:T(8,128)(2,1)} %bitcast.175) | data formatting | bytes 12582912 | tf_op jit(solution)/shard_map/all_to_all | solution.py:120
  (151 shorter events, 27.3 us)
Async XLA Ops:
  6.5 3.7 copy-start.2
  6.5 8.6 %copy-start.4 = (f32[4,2048]{1,0:T(4,128)S(1)}, f32[4,2048]{1,0:T(4,128)}, u32[]{:S(2)}) copy-start(f32[4,2048]{1,0:T(4,128)} %param.19) | copy-start | bytes 98308
  6.5 8.6 %copy-start.6 = (f32[4,2,256]{2,1,0:T(2,128)S(1)}, f32[4,2,256]{2,1,0:T(2,128)}, u32[]{:S(2)}) copy-start(f32[4,2,256]{2,1,0:T(2,128)} %param.20) | copy-start | bytes 24580
  6.5 8.6 %copy-start.7 = (f32[2,32]{1,0:T(2,128)S(1)}, f32[2,32]{1,0:T(2,128)}, u32[]{:S(2)}) copy-start(f32[2,32]{1,0:T(2,128)} %param.21) | copy-start | bytes 772
  6.5 8.6 %copy-start.3 = (f32[1536,32]{0,1:T(8,128)S(1)}, f32[1536,32]{0,1:T(8,128)}, u32[]{:S(2)}) copy-start(f32[1536,32]{0,1:T(8,128)} %param.18) | copy-start | bytes 589828
  6.5 305.4 %all-gather.5.cloned.1.call-start = ((), (), s32[]{:S(2)}) async-start(), calls=%async_computation.1 | async-start | bytes 9437184 | tf_op jit(solution)/shard_map/all_gather | solution.py:24
  10.7 3.1 copy-start.1
  13.8 5.7 %collective-permute-start = (bf16[3,2560]{1,0:T(4,128)(2,1)S(1)}, bf16[3,2560]{1,0:T(4,128)(2,1)S(1)}, u32[]{:S(2)}, u32[]{:S(2)}) collective-permute-start(bf16[3,2560]{1,0:T(4,128)(2,1)S(1)} %slice.73), channel_id=1, source_target_pairs={{0,4},{4,8},{8,12},{12,16},{16,20},{20,24},{24,28},{1,5},{5,9},{9,... | collective-permute-start | bytes 46088 | tf_op jit(solution)/shard_map/ppermute | solution.py:19
  188.1 1.0 copy-start
  207.1 16.0 %copy-start.8 = (f32[32]{0:T(128)S(1)}, f32[32]{0:T(128)}, u32[]{:S(2)}) copy-start(f32[32]{0:T(128)} %param.22) | copy-start | bytes 388
  366.1 17.2 %copy-start.5 = (f32[2048]{0:T(1024)S(1)}, f32[2048]{0:T(1024)}, u32[]{:S(2)}) copy-start(f32[2048]{0:T(1024)} %param.23) | copy-start | bytes 24580
Sparse Core Ops, SparseCore 0:
  189.3 122.6 all-gather.4
where the time goes:
time: 489 us; the launch traced here: 483 us
  local copies, waits for them, and re-layouts  149 us (30%)
  blocking collectives  90.7 us (19%)
  other arithmetic  87.2 us (18%)
  waiting for transfers between devices  73.9 us (15%)
  matrix products  65.8 us (13%)
  between operations  13.8 us (3%)
    all_to_all x1, blocking collectives, per_device(): lax.all_to_all(normed, 'head', split_axis=0, concat_axis=1, tiled=True)  74.2 us
    all_gather x1, waiting for transfers between devices, entering_2(): gathered = jax.tree.map(lambda a: lax.all_gather(a, axis), part)  71.4 us
    unnamed x24, local copies, waits for them, and re-layouts  33.8 us
    dot_general x6, matrix products, stretch_terms(): jnp.einsum('tsgh,sghp->tghp', weights, values, preferred_element_type=jnp...  26.9 us
    convert_element_type x1, other arithmetic, per_device(): conved = jax.nn.silu(summed).astype(jnp.bfloat16)  22.1 us
    dot_general x1, matrix products, per_device(): jnp.einsum('ctgn,cghpn->ctghp', c_wide, entering, precision=HIGHEST_PRECI...  21.7 us
    add x1, local copies, waits for them, and re-layouts, per_device(): inside + from_state + skipped  21.7 us
    reshape x1, local copies, waits for them, and re-layouts, per_device(): conved[:, :channel_count]  18.6 us
  transfers between devices with their start and end apart: 2, of which 2 were waited for; matrix products, arithmetic and copies ran while one was open for 8% of the time, Pallas kernels for 0%

commit v1 on v0

v1 whole, which is shorter than its diff:
```python
import functools
import math

import jax
import jax.numpy as jnp
import numpy as np
from jax import lax
from jax.experimental import pallas as pl
from jax.experimental.pallas import tpu as pltpu
from jax.sharding import PartitionSpec as P


HEAD_DIM = 64
STATE = 128
TAPS = 4
LANES = 128
SUB = 64
EPSILON = 1e-05
LOG2E = 1.0 / math.log(2.0)
HIGHEST = lax.Precision.HIGHEST
F32 = jnp.float32
BF16 = jnp.bfloat16
STATES_STEP = 3
SMALL_LIMIT = 8 * 1024 * 1024
VMEM_LIMIT = 60 * 1024 * 1024


def dot(a, b, dims=((1,), (0,)), precision=None):
    return lax.dot_general(a, b, (dims, ((), ())), precision=precision, preferred_element_type=F32)


def silu(v):
    half = 0.5 * v
    return half + half * jnp.tanh(half)


def params(n_dims):
    return pltpu.CompilerParams(
        dimension_semantics=("arbitrary",) * n_dims, vmem_limit_bytes=VMEM_LIMIT
    )


def cost(flops, bytes_accessed, transcendentals=0):
    return pl.CostEstimate(
        flops=int(flops), bytes_accessed=int(bytes_accessed), transcendentals=int(transcendentals)
    )


def prep_kernel(
    q, groups, step_ref, rates_ref, gains_ref, choose_ref,
    split_ref, spread_ref, rel_ref, before_ref, reach_ref, skip_ref, held,
):
    heads, rows = step_ref.shape
    upper = (
        lax.broadcasted_iota(jnp.int32, (q, q), 0) <= lax.broadcasted_iota(jnp.int32, (q, q), 1)
    ).astype(F32)
    lane = lax.broadcasted_iota(jnp.int32, (heads, LANES), 1)
    rates = jnp.transpose(jnp.concatenate([rates_ref[...], jnp.zeros((6, heads), F32)], 0))
    raw = step_ref[...] + rates[:, 0:1]
    step = jnp.maximum(raw, 0.0) + jnp.log1p(jnp.exp(-jnp.abs(raw)))
    rated = -LOG2E * jnp.exp(rates[:, 1:2]) * step
    shift = jnp.log(step) * LOG2E
    blocks = rows // q
    stacked = jnp.concatenate([rated[:, k * q : (k + 1) * q] for k in range(blocks)], 0)
    summed = dot(stacked, upper, precision=HIGHEST)
    before = jnp.zeros((heads, 1), F32)
    befores = jnp.zeros((heads, LANES), F32)
    for k in range(blocks):
        cum = summed[k * heads : (k + 1) * heads]
        final = cum[:, q - 1 : q]
        rel = cum - shift[:, k * q : (k + 1) * q]
        held[k] = rel
        even = held[k, pl.ds(0, heads // 2, stride=2), :]
        odd = held[k, pl.ds(1, heads // 2, stride=2), :]
        for j in range(q // SUB):
            part = slice(j * SUB, (j + 1) * SUB)
            rel_ref[k, j] = jnp.concatenate([even[:, part], odd[:, part]], 1)
        per_group = heads // groups
        cuts = [slice(g * per_group, (g + 1) * per_group) for g in range(groups)]
        parts = []
        for value in (jnp.exp2(final - rel), jnp.exp2(cum)):
            high = value.astype(BF16).astype(F32)
            parts += [high, value - high]
        parts = [part[cut] for cut in cuts for part in parts]
        rows_k = slice(k * q, (k + 1) * q)
        spread_ref[rows_k, :] = jnp.transpose(jnp.concatenate(parts, 0)).astype(BF16)
        high = cum.astype(BF16).astype(F32)
        middle = (cum - high).astype(BF16).astype(F32)
        parts = [high, middle, cum - high - middle, jnp.zeros_like(cum)]
        parts = [part[cut] for cut in cuts for part in parts]
        split_ref[rows_k, :] = jnp.transpose(jnp.concatenate(parts, 0)).astype(BF16)
        befores = jnp.where(lane == k, before, befores)
        before = before + final
    befores = jnp.where(lane == blocks, before, befores)
    before_ref[...] = jnp.transpose(befores)[: blocks + 1]
    by_head = jnp.concatenate([jnp.exp2(before_ref[...]), gains_ref[...]], 0)
    reach = dot(by_head, choose_ref[...], precision=HIGHEST)
    skip_ref[...] = reach[blocks + 1 :]
    for k in range(blocks + 1):
        reach_ref[k] = reach[k : k + 1]


def prep(step_raw, head_rates, skip_gain, q, groups):
    rows, heads = step_raw.shape
    blocks = rows // q
    choose = jnp.asarray(np.repeat(np.eye(heads, dtype=np.float32), HEAD_DIM, axis=1))
    return pl.pallas_call(
        functools.partial(prep_kernel, q, groups),
        out_shape=(
            jax.ShapeDtypeStruct((rows, 4 * heads), BF16),
            jax.ShapeDtypeStruct((rows, 4 * heads), BF16),
            jax.ShapeDtypeStruct((blocks, q // SUB, heads // 2, 2 * SUB), F32),
            jax.ShapeDtypeStruct((blocks + 1, heads), F32),
            jax.ShapeDtypeStruct((blocks + 1, 1, heads * HEAD_DIM), F32),
            jax.ShapeDtypeStruct((1, heads * HEAD_DIM), F32),
        ),
        scratch_shapes=[pltpu.VMEM((blocks, heads, q), F32)],
        compiler_params=pltpu.CompilerParams(vmem_limit_bytes=VMEM_LIMIT),
        cost_estimate=cost(rows * q * heads * 12, rows * heads * 16, rows * heads * 4),
        name="prep",
    )(step_raw.T, head_rates, skip_gain[None, :], choose)


def choice(per_group):
    one = np.repeat(np.eye(per_group, dtype=np.float32), HEAD_DIM, axis=1)
    return jnp.asarray(np.concatenate([one] * 3, 0), BF16)


def states_kernel(
    group, groups, pieces, q, starts, ends,
    x_ref, maps_ref, spread_ref, halo_ref, taps_x_ref, taps_m_ref, before_ref, choose_ref, *rest,
):
    xc_ref, mc_ref, local_ref, final_ref, carry_ref, buffer, last, state, weight, tail = rest[-10:]
    step = pl.program_id(0)
    width = x_ref.shape[1]
    heads = before_ref.shape[1]
    per_group = heads // groups
    channels = groups * width
    tiles = width // LANES
    sources = [(group * width + p * LANES) for p in range(tiles)]
    sources += [channels + group * STATE, channels + (groups + group) * STATE]

    @pl.when(step == 0)
    def _():
        if starts:
            for t, column in enumerate(sources):
                last[t] = halo_ref[:, column : column + LANES].astype(F32)
            state[...] = jnp.zeros_like(state)
        else:
            state[...] = rest[0][:STATE, :]
            for t in range(len(sources)):
                if t < tiles:
                    last[t] = rest[0][STATE : STATE + 8, t * LANES : (t + 1) * LANES]
                else:
                    place = (t - tiles) * LANES
                    last[t] = rest[0][STATE + 8 :, place : place + LANES]

    def conv(t, raw, taps):
        rows = buffer.at[t]
        rows[0:8, :] = last[t]
        rows[8 : 8 + q, :] = raw.astype(F32)
        half = taps[0:1, :] * rows[5 : 5 + q, :]
        for i in range(1, TAPS):
            half = half + taps[i : i + 1, :] * rows[5 + i : 5 + i + q, :]
        last[t] = rows[q : q + 8, :]
        return (half + half * jnp.tanh(half)).astype(BF16)

    def block(i):
        rows = pl.ds(pl.multiple_of(i * q, q), q)
        parts = group * 4 * per_group
        choose = choose_ref[: 2 * per_group, :]
        weight[...] = dot(spread_ref[rows, parts : parts + 2 * per_group], choose)
        for m in range(2):
            column = (m * groups + group) * STATE
            taps = 0.5 * taps_m_ref[:, m, group * STATE : (group + 1) * STATE]
            mc_ref[rows, m * STATE : (m + 1) * STATE] = conv(
                tiles + m, maps_ref[rows, column : column + STATE], taps
            )
        for p in range(tiles):
            cols = slice(p * LANES, (p + 1) * LANES)
            first = group * width + p * LANES
            xc = conv(p, x_ref[rows, cols], 0.5 * taps_x_ref[:, first : first + LANES])
            xc_ref[rows, cols] = xc
            tail[:, cols] = (weight[:, cols] * xc.astype(F32)).astype(BF16)
        tip = pl.ds(pl.multiple_of(i * q + q - 16, 16), 16)
        decay = dot(spread_ref[tip, parts + 2 * per_group : parts + 4 * per_group], choose)[15:16]
        held = state[...]
        local_ref[i] = held.astype(BF16)
        state[...] = decay * held + dot(jnp.transpose(mc_ref[rows, :STATE]), tail[...])

    pl.loop(0, x_ref.shape[0] // q)(block)

    @pl.when(step == pl.num_programs(0) - 1)
    def _():
        if not ends:
            carry_ref[:STATE, :] = state[...]
            for t in range(len(sources)):
                if t < tiles:
                    carry_ref[STATE : STATE + 8, t * LANES : (t + 1) * LANES] = last[t]
                else:
                    place = (t - tiles) * LANES
                    carry_ref[STATE + 8 :, place : place + LANES] = last[t]
            return
        payload_ref = final_ref
        payload_ref[:, :width] = state[...].astype(BF16)
        blocks = before_ref.shape[0] - 1
        first = group * per_group
        decay = jnp.exp2(before_ref[blocks : blocks + 1, :])[:, first : first + per_group]
        high = decay.astype(BF16).astype(F32)
        low = decay - high
        place = lax.broadcasted_iota(jnp.int32, (STATE, per_group), 0) % (STATE // pieces)
        extra = jnp.where(place == 0, high, jnp.where(place == 1, low, 0.0))
        payload_ref[:, width:] = jnp.concatenate(
            [extra, jnp.zeros((STATE, LANES - per_group), F32)], 1
        ).astype(BF16)


def whole(shape):
    return pl.BlockSpec(shape, lambda *_: (0,) * len(shape))


def states(group, groups, pieces, q, first, last, x, maps, halo, taps_x, taps_maps, spread_log,
           before, earlier=None):
    rows, channels = x.shape
    heads = before.shape[1]
    width = channels // groups
    blocks = rows // q
    starts, ends = first == 0, last == blocks
    step = math.gcd(STATES_STEP, math.gcd(first, last))
    skip = first // step

    in_specs = [
        pl.BlockSpec((step * q, width), lambda k: (skip + k, group)),
        pl.BlockSpec((step * q, maps.shape[1]), lambda k: (skip + k, 0)),
        pl.BlockSpec((step * q, 4 * heads), lambda k: (skip + k, 0)),
    ]
    operands = [
        x, maps, spread_log, halo, taps_x, taps_maps, before,
        choice(heads // groups),
    ]
    in_specs += [whole(a.shape) for a in operands[3:]]
    aliases = {}
    if earlier is not None:
        in_specs += [whole(earlier[4].shape)] + [pl.BlockSpec(memory_space=pl.ANY)] * 3
        operands += [earlier[4], *earlier[:3]]
        aliases = {len(operands) - 3 + i: i for i in range(3)}
    final = (STATE, width + LANES) if ends else (8, LANES)
    carry = (8, LANES) if ends else (STATE + 16, width)
    return pl.pallas_call(
        functools.partial(states_kernel, group, groups, pieces, q, starts, ends),
        grid=((last - first) // step,),
        in_specs=in_specs,
        out_specs=[
            pl.BlockSpec((step * q, width), lambda k: (skip + k, 0)),
            pl.BlockSpec((step * q, 2 * STATE), lambda k: (skip + k, 0)),
            pl.BlockSpec((step, STATE, width), lambda k: (skip + k, 0, 0)),
            pl.BlockSpec(final, lambda k: (0, 0)),
            pl.BlockSpec(carry, lambda k: (0, 0)),
        ],
        out_shape=(
            jax.ShapeDtypeStruct((rows, width), BF16),
            jax.ShapeDtypeStruct((rows, 2 * STATE), BF16),
            jax.ShapeDtypeStruct((blocks, STATE, width), BF16),
            jax.ShapeDtypeStruct(final, BF16),
            jax.ShapeDtypeStruct(carry, F32),
        ),
        input_output_aliases=aliases,
        scratch_shapes=[
            pltpu.VMEM((2 + width // LANES, q + 8, LANES), F32),
            pltpu.VMEM((2 + width // LANES, 8, LANES), F32),
            pltpu.VMEM((STATE, width), F32),
            pltpu.VMEM((q, width), F32),
            pltpu.VMEM((q, width), BF16),
        ],
        compiler_params=params(1),
        cost_estimate=cost(
            2 * (last - first) * q * STATE * width,
            8 * (last - first) * q * width,
            3 * (last - first) * q * width,
        ),
        name="states",
    )(*operands)


def spread(width):
    row = lax.broadcasted_iota(jnp.int32, (LANES, width), 0)
    col = lax.broadcasted_iota(jnp.int32, (LANES, width), 1)
    return (col // HEAD_DIM == row).astype(BF16)


def scan_kernel(part_ref, out_ref):
    pieces, _, wide = part_ref.shape
    width = wide - LANES
    high = jnp.concatenate([part_ref[j, 0:1, width:] for j in range(pieces)], 0)
    low = jnp.concatenate([part_ref[j, 1:2, width:] for j in range(pieces)], 0)
    one_hot = spread(width)
    decay = dot(high, one_hot) + dot(low, one_hot)
    state = jnp.zeros(out_ref.shape[1:], F32)
    for j in range(pieces):
        out_ref[j] = state.astype(BF16)
        state = decay[j : j + 1, :] * state + part_ref[j, :, :width].astype(F32)


def scan_shards(part):
    pieces, depth, wide = part.shape
    return pl.pallas_call(
        scan_kernel,
        out_shape=jax.ShapeDtypeStruct((pieces, depth, wide - LANES), BF16),
        compiler_params=pltpu.CompilerParams(vmem_limit_bytes=SMALL_LIMIT),
        cost_estimate=cost(4 * pieces * depth * wide, 4 * pieces * depth * wide),
        name="scan_shards",
    )(part)


def outputs_kernel(
    group, near,
    where_ref, x_ref, maps_ref, gate_ref, split_ref, rel_ref, spread_ref, reach_ref, local_ref,
    enter_ref, choose_ref, gain_ref, skip_ref, *rest,
):
    held, logs = rest[-2:]
    q, width = x_ref.shape
    tiles = width // LANES
    subs = q // SUB
    row = lax.broadcasted_iota(jnp.int32, (SUB, LANES), 0)
    lane = lax.broadcasted_iota(jnp.int32, (SUB, LANES), 1)
    causal = row >= lane % SUB
    left = lane < HEAD_DIM
    zero = jnp.zeros((SUB, LANES), BF16)
    c_now = maps_ref[:, STATE:]
    scores = []
    for j in range(subs):
        b_now = maps_ref[j * SUB : (j + 1) * SUB, :STATE]
        twice = jnp.concatenate([b_now, b_now], 0)
        scores.append(dot(c_now[j * SUB :], twice, ((1,), (1,))))
    wide = min(width, 2 * LANES)
    per_group = width // HEAD_DIM
    parts = group * 4 * per_group
    grown = spread_ref[:, parts + 2 * per_group : parts + 4 * per_group]
    split = split_ref[:, parts : parts + 3 * per_group]
    for first in range(0, width, wide):
        cols = slice(first, first + wide)
        held[:, cols] = reach_ref[0, :, cols] * dot(c_now, enter_ref[:, cols])
        held[:, cols] = held[:, cols] + dot(c_now, local_ref[0, :, cols])
        held[:, cols] = held[:, cols] * dot(grown, choose_ref[: 2 * per_group, cols])
        logs[:, cols] = dot(split, choose_ref[:, cols])
    squares = [jnp.zeros((SUB, LANES), F32) for _ in range(subs)]
    for p in range(tiles):
        cols = slice(p * LANES, (p + 1) * LANES)
        stacked = []
        for i in range(subs):
            rows = slice(i * SUB, (i + 1) * SUB)
            x_now = x_ref[rows, cols]
            stacked += [jnp.where(left, x_now, zero), jnp.where(left, zero, x_now)]
            weights = []
            for j in range(i + 1):
                decay = jnp.exp2(logs[rows, cols] - rel_ref[0, j, group * tiles + p, :][None, :])
                weight = scores[j][(i - j) * SUB : (i - j + 1) * SUB] * decay
                weights.append((jnp.where(causal, weight, 0.0) if i == j else weight).astype(BF16))
            total = held[rows, cols] + skip_ref[:, cols] * x_now.astype(F32)
            total = total + dot(jnp.concatenate(weights, 1), jnp.concatenate(stacked, 0))
            total = total * silu(gate_ref[rows, cols].astype(F32))
            held[rows, cols] = total
            squares[i] = squares[i] + total * total

    def store(out_ref):
        for i in range(subs):
            rows = slice(i * SUB, (i + 1) * SUB)
            mean = jnp.sum(squares[i], axis=1, keepdims=True) * (1.0 / width)
            inverse = lax.rsqrt(mean + EPSILON)
            for p in range(tiles):
                cols = slice(p * LANES, (p + 1) * LANES)
                out_ref[rows, cols] = (held[rows, cols] * inverse * gain_ref[:, cols]).astype(BF16)

    if near:
        pl.when(pl.program_id(0) < near)(lambda: store(rest[-4]))
        pl.when(pl.program_id(0) >= near)(lambda: store(rest[-3]))
    else:
        store(rest[-3])


def outputs(group, groups, q, far, first, count, span, me, conved, logs, enter, gate, gain,
            token=None, target=None):
    xc, mc, local = conved
    split, spread_log, rel, before, reach, skip = logs
    _, width = xc.shape
    heads = before.shape[1]
    blocks = span // q
    home = target is not None and far > 0
    own = target is not None and far == 0

    def at(i, s):
        if home:
            return (s[0] ^ jnp.where(i < blocks, 1, 0)) * blocks + lax.rem(i, blocks)
        return (s[0] ^ far) * blocks + first + i

    in_specs = [
        pl.BlockSpec((q, width), lambda i, s: (at(i, s), 0)),
        pl.BlockSpec((q, 2 * STATE), lambda i, s: (at(i, s), 0)),
        pl.BlockSpec((q, width), lambda i, s: (at(i, s), group)),
        pl.BlockSpec((q, 4 * heads), lambda i, s: (at(i, s), 0)),
        pl.BlockSpec((1, q // SUB, heads // 2, LANES), lambda i, s: (at(i, s), 0, 0, 0)),
        pl.BlockSpec((q, 4 * heads), lambda i, s: (at(i, s), 0)),
        pl.BlockSpec((1, 1, width), lambda i, s: (at(i, s), 0, group)),
        pl.BlockSpec((1, STATE, width), lambda i, s: (at(i, s), 0, 0)),
        whole((STATE, width)),
        whole((3 * width // HEAD_DIM, width)),
        pl.BlockSpec((1, width), lambda i, s: (0, group)),
        pl.BlockSpec((1, width), lambda i, s: (0, group)),
    ]
    operands = [
        xc, mc, gate, split, rel, spread_log, reach, local,
        enter, choice(heads // groups), gain, skip,
    ]
    if token is not None:
        in_specs.append(pl.BlockSpec(memory_space=pl.ANY))
        operands.append(token)
    aliases = {}
    if home or own:
        start = blocks if home else 0
        count = start + blocks
        out_shape, out_specs = [], []
        if home:
            out_shape.append(jax.ShapeDtypeStruct((span, width), BF16))
            out_specs.append(pl.BlockSpec((q, width), lambda i, s: (jnp.minimum(i, blocks - 1), 0)))
        out_specs.append(
            pl.BlockSpec((q, width), lambda i, s: (jnp.maximum(i - start, 0), s[0] * groups + group))
        )
        if isinstance(target, tuple):
            out_shape.append(jax.ShapeDtypeStruct(target, BF16))
        else:
            out_shape.append(jax.ShapeDtypeStruct(target.shape, BF16))
            in_specs.append(pl.BlockSpec(memory_space=pl.ANY))
            operands.append(target)
            aliases = {len(operands): len(out_shape) - 1}
    else:
        out_shape = jax.ShapeDtypeStruct((count * q, width), BF16)
        out_specs = pl.BlockSpec((q, width), lambda i, s: (i, 0))
    return pl.pallas_call(
        functools.partial(outputs_kernel, group, blocks if home else 0),
        grid_spec=pltpu.PrefetchScalarGridSpec(
            num_scalar_prefetch=1,
            grid=(count,),
            in_specs=in_specs,
            out_specs=out_specs,
            scratch_shapes=[pltpu.VMEM((q, width), F32)] * 2,
        ),
        out_shape=out_shape,
        input_output_aliases=aliases,
        compiler_params=params(1),
        cost_estimate=cost(
            count * q * width * (2 * STATE + 4 * q), 8 * count * q * width, count * q * width * 4
        ),
        name="outputs",
    )(me, *operands)


def place_kernel(places, width, me_ref, *refs):
    count = len(places)
    out_ref, held, taken, put = refs[count + 1 :]
    copies = []
    at = 0
    for i, (far, group, groups, first, rows) in enumerate(places):
        slot = held.at[pl.ds(at, rows), :]
        column = pl.multiple_of(((me_ref[0] ^ far) * groups + group) * width, width)
        into = out_ref.at[pl.ds(first, rows), pl.ds(column, width)]
        copies.append(
            (
                pltpu.make_async_copy(refs[i], slot, taken.at[i]),
                pltpu.make_async_copy(slot, into, put.at[i]),
            )
        )
        at += rows
    for take, _ in copies:
        take.start()
    for take, give in copies:
        take.wait()
        give.start()
    for _, give in copies:
        give.wait()


def place(target, blocks, places, me):
    width = blocks[0].shape[1]
    total = sum(block.shape[0] for block in blocks)
    count = len(blocks)
    return pl.pallas_call(
        functools.partial(place_kernel, places, width),
        in_specs=[pl.BlockSpec(memory_space=pltpu.SMEM)]
        + [pl.BlockSpec(memory_space=pl.ANY)] * (count + 1),
        out_specs=pl.BlockSpec(memory_space=pl.ANY),
        out_shape=jax.ShapeDtypeStruct(target.shape, target.dtype),
        scratch_shapes=[
            pltpu.VMEM((total, width), BF16),
            pltpu.SemaphoreType.DMA((count,)),
            pltpu.SemaphoreType.DMA((count,)),
        ],
        input_output_aliases={count + 1: 0},
        compiler_params=pltpu.CompilerParams(vmem_limit_bytes=SMALL_LIMIT),
        cost_estimate=cost(0, 4 * total * width),
        name="place",
    )(me, *blocks, target)


def per_device(
    channels_in,
    state_maps,
    gate_in,
    step_raw,
    convolution_channel_taps,
    conv_maps,
    head_rates,
    skip_gain,
    norm_gain,
):
    rows, channels = channels_in.shape
    heads = step_raw.shape[1]
    map_width = state_maps.shape[2]
    groups = map_width // STATE
    width = heads // groups * HEAD_DIM
    shards = lax.axis_size("ctx")
    peers = lax.axis_size("head")
    me = lax.axis_index("head").reshape(1)
    span = rows // peers
    q = LANES if span % LANES == 0 else HEAD_DIM

    maps = state_maps.reshape(rows, 2 * map_width)
    ahead = [(i, i + 1) for i in range(shards - 1)]
    edge = jnp.concatenate([channels_in[rows - 8 :], maps[rows - 8 :]], 1)
    halo = lax.ppermute(edge, "ctx", ahead)

    logs = prep(step_raw, head_rates, skip_gain, q, groups)
    gain = norm_gain[None, :]

    def shard_states(group):
        blocks = rows // q
        cuts = [0, blocks] if group == 0 else [0, blocks // 2, blocks]
        done = None
        for first, last in zip(cuts[:-1], cuts[1:]):
            done = states(
                group, groups, shards, q, first, last, channels_in, maps, halo,
                convolution_channel_taps, conv_maps, logs[1], logs[3], done,
            )
        return done[:3], done[3].reshape(shards, STATE // shards, width + LANES)

    def exchange(payload):
        return lax.all_to_all(payload, "ctx", 0, 0, tiled=True)

    def block_of(group, far, first, count, **more):
        return outputs(
            group, groups, q, far, first, count, span, me, conved[group], logs, entering[group],
            gate_in, gain, **more,
        )

    def send(block, far):
        return lax.ppermute(block, "head", [(i, i ^ far) for i in range(peers)])

    conved, payloads = zip(*[shard_states(group) for group in range(groups)])
    entering, arrived, tokens = [], [], []
    blocks = span // q
    result = (span, channels * peers)
    for group in range(groups):
        payload = payloads[group]
        if group > 0:
            payload, _ = lax.optimization_barrier((payload, tokens[1]))
        part = exchange(payload)
        part = scan_shards(part)
        entering.append(exchange(part).reshape(STATE, width))
        for far in range(peers - 1, 1, -1):
            for first, last in sends(group, groups, far, peers, blocks):
                block = block_of(
                    group, far, first, last - first, token=tokens[-1] if tokens else None
                )
                tokens.append(block)
                arrived.append((send(block, far), (far, group, groups, first * q, (last - first) * q)))
        if group < groups - 1:
            home = block_of(group, 1, 0, blocks, token=tokens[-1])
            arrived.append((send(home, 1), (1, group, groups, 0, span)))
    for group in range(groups):
        if group < groups - 1:
            (result,) = block_of(group, 0, 0, blocks, token=tokens[-1], target=result)
        else:
            home, result = block_of(group, 1, 0, blocks, token=tokens[-1], target=result)
    arrived.append((send(home, 1), (1, groups - 1, groups, 0, span)))
    arrived.sort(key=lambda a: (a[1][1] == groups - 1 and a[1][0] > 1))
    late = sum(a[1][1] == groups - 1 and a[1][0] > 1 for a in arrived)
    cuts = [0, len(arrived) - late, len(arrived) - 1, len(arrived)]
    for low, high in zip(cuts[:-1], cuts[1:]):
        if high > low:
            part = arrived[low:high]
            result = place(result, [a[0] for a in part], [a[1] for a in part], me)
    return result


def sends(group, groups, far, peers, blocks):
    if blocks > 1 and far == peers - 1:
        return [(0, 1), (1, blocks)]
    if blocks > 1 and group == groups - 1 and far == 2:
        return [(0, blocks - 1), (blocks - 1, blocks)]
    return [(0, blocks)]


def solution(mesh):
    return jax.shard_map(
        per_device,
        mesh=mesh,
        in_specs=(
            P("ctx", "head"),
            P("ctx", None, "head"),
            P("ctx", "head"),
            P("ctx", "head"),
            P(None, "head"),
            P(None, None, "head"),
            P(None, "head"),
            P("head"),
            P("head"),
        ),
        out_specs=P(("ctx", "head"), None),
        check_vma=False,
    )
```

time: 489 us -> 171 us (0.35)
  local copies, waits for them, and re-layouts: 149 us -> 6.37 us
  other arithmetic: 87.2 us -> 0.01 us
  Pallas kernels: 0 us -> 77.6 us
  matrix products: 65.8 us -> 0 us
  blocking collectives: 90.7 us -> 25.7 us
  waiting for transfers between devices: 73.9 us -> 36.6 us
  starting transfers between devices: 1.33 us -> 21.4 us
  between operations: 13.8 us -> 0.29 us
    pallas_call x0 -> x19, Pallas kernels: none -> 77.6 us  [the longest x10 43.6 us: outputs(): pl.pallas_call(functools.partial(outputs_kernel, group, blocks if home el...]
    all_gather x1 -> x0, waiting for transfers between devices: 71.4 us -> none  [entering_2(): gathered = jax.tree.map(lambda a: lax.all_gather(a, axis), part)]
    dot_general x19 -> x0, matrix products: 65.8 us -> none  [the longest x6 26.9 us: stretch_terms(): jnp.einsum('tsgh,sghp->tghp', weights, values, preferred_element_type=jnp...]
    all_to_all x1 -> x2, blocking collectives: 74.2 us -> 25.7 us  [exchange(): return lax.all_to_all(payload, 'ctx', 0, 0, tiled=True)]
    convert_element_type x3 -> x0, other arithmetic: 42.4 us -> none  [the longest x1 22.1 us: per_device(): conved = jax.nn.silu(summed).astype(jnp.bfloat16)]
    reshape x12 -> x0, local copies, waits for them, and re-layouts: 39.2 us -> none  [the longest x1 18.6 us: per_device(): conved[:, :channel_count]]
    ppermute x1 -> x10, waiting for transfers between devices: 2.46 us -> 36.6 us  [the longest x9 36.6 us: send(): return lax.ppermute(block, 'head', [(i, i ^ far) for i in range(peers)])]
    unnamed x24 -> x21, local copies, waits for them, and re-layouts: 33.8 us -> 5.61 us
  transfers between devices with their start and end apart: 2 -> 12, of which waited for: 2 -> 3; matrix products, arithmetic and copies ran while one was open for 8% -> 2% of each run, Pallas kernels for 0% -> 34%
where the time goes in v1:
time: 171 us; the launch traced here: 168 us
  Pallas kernels  77.6 us (45%)
  waiting for transfers between devices  36.6 us (21%)
  blocking collectives  25.7 us (15%)
  starting transfers between devices  21.4 us (13%)
  local copies, waits for them, and re-layouts  6.37 us (4%)
    pallas_call x10, Pallas kernels, outputs(): pl.pallas_call(functools.partial(outputs_kernel, group, blocks if home el...  43.6 us
    ppermute x9, waiting for transfers between devices, send(): return lax.ppermute(block, 'head', [(i, i ^ far) for i in range(peers)])  36.6 us
    all_to_all x2, blocking collectives, exchange(): return lax.all_to_all(payload, 'ctx', 0, 0, tiled=True)  25.7 us
    pallas_call x3, Pallas kernels, states(): pl.pallas_call(functools.partial(states_kernel, group, groups, pieces, q,...  24.9 us
    all_to_all x2, starting transfers between devices, exchange(): return lax.all_to_all(payload, 'ctx', 0, 0, tiled=True)  13 us
    ppermute x9, starting transfers between devices, send(): return lax.ppermute(block, 'head', [(i, i ^ far) for i in range(peers)])  7.06 us
    unnamed x21, local copies, waits for them, and re-layouts  5.61 us
    pallas_call x3, Pallas kernels, place(): pl.pallas_call(functools.partial(place_kernel, places, width), in_specs=[...  3.89 us
  transfers between devices with their start and end apart: 12, of which 3 were waited for; matrix products, arithmetic and copies ran while one was open for 2% of the time, Pallas kernels for 34%

profile of v1, /device:TPU:26, one launch (start us, length us, event | category | flops | bytes accessed | tf_op | source)
XLA Modules:
  0.0 168.0 jit_solution(9722715021811712643)
XLA Ops:
  0.0 0.7 slice_bitcast_fusion
  0.7 0.8 slice.9
  1.5 1.3 collective-permute-start
  2.8 2.9 %copy.31 = bf16[192,8,2,256]{3,1,2,0:T(8,128)(2,1)} copy(bf16[192,8,2,256]{3,2,1,0:T(2,128)(2,1)} %bitcast.26) | data formatting | bytes 3145728
  5.6 3.4 %prep.1 = (bf16[1536,128]{1,0:T(8,128)(2,1)}, bf16[1536,128]{1,0:T(8,128)(2,1)}, f32[12,2,16,128]{3,2,1,0:T(8,128)}, f32[13,32]{1,0:T(8,128)}, f32[13,1,2048]{2,1,0:T(1,128)}, /*index=5*/f32[1,2048]{1,0:T(1,128)}) custom-call(f32[32,1536]{1,0:T(8,128)} %bitcast.39, f32[2,32]{1,0:T(2,128)} %rates_ref.1, f32[1,32]{1,0:T(1,128)} %bitcast.41, ...), custom_call_target="tpu_custom_call" | custom-call | flops 75497472 | bytes 786432 | tf_op jit(solution)/shard_map/prep/pallas_call | solution.py:107
  9.0 0.0 collective-permute-done.halo_ref
  9.0 0.0 copy-start.8
  9.0 0.6 copy-done.8
  9.6 10.7 %states.5 = (bf16[1536,1024]{1,0:T(8,128)(2,1)}, bf16[1536,256]{1,0:T(8,128)(2,1)}, bf16[12,128,1024]{2,1,0:T(8,128)(2,1)}, bf16[128,1152]{1,0:T(8,128)(2,1)}, f32[8,128]{1,0:T(8,128)}) custom-call(bf16[1536,2048]{1,0:T(8,128)(2,1)} %x_ref.5, bf16[1536,512]{1,0:T(8,128)(2,1)} %bitcast.13, bf16[1536,128]{1,0:T(8,128)(2,1)} %get-tuple-element.26.spread_ref, ...), custom_call_target="tpu_custom_call" | custom-call | flops 402653184 | bytes 12582912 | tf_op jit(solution)/shard_map/states/pallas_call | solution.py:249
  20.3 14.1 %all_to_all.20.part_ref = bf16[8,16,1152]{2,1,0:T(8,128)(2,1)S(1)} all-to-all(bf16[8,16,1152]{2,1,0:T(8,128)(2,1)} %bitcast.38), channel_id=1, replica_groups=mesh['ctx'=8,'head'=4] {'ctx'}, dimensions={0} | all-to-all | bytes 589824 | tf_op jit(solution)/shard_map/all_to_all | solution.py:546
  34.4 0.9 scan_shards.2
  35.4 6.5 %all-to-all-start.1 = ((bf16[8,16,1024]{2,1,0:T(8,128)(2,1)}), bf16[8,16,1024]{2,1,0:T(8,128)(2,1)S(1)}, u32[]{:S(2)}, u32[]{:S(2)}) async-start(bf16[8,16,1024]{2,1,0:T(8,128)(2,1)} %scan_shards.2), calls=%async_computation.1 | async-start | bytes 524288 | tf_op jit(solution)/shard_map/all_to_all | solution.py:546
  41.9 7.0 %states.3 = (bf16[1536,1024]{1,0:T(8,128)(2,1)}, bf16[1536,256]{1,0:T(8,128)(2,1)}, bf16[12,128,1024]{2,1,0:T(8,128)(2,1)}, bf16[8,128]{1,0:T(8,128)(2,1)}, f32[144,1024]{1,0:T(8,128)}) custom-call(bf16[1536,2048]{1,0:T(8,128)(2,1)} %x_ref.5, bf16[1536,512]{1,0:T(8,128)(2,1)} %bitcast.14, bf16[1536,128]{1,0:T(8,128)(2,1)} %get-tuple-element.26.spread_ref, ...), custom_call_target="tpu_custom_call" | custom-call | flops 201326592 | bytes 6291456 | tf_op jit(solution)/shard_map/states/pallas_call | solution.py:249
  48.9 7.2 %states.4 = (bf16[1536,1024]{1,0:T(8,128)(2,1)}, bf16[1536,256]{1,0:T(8,128)(2,1)}, bf16[12,128,1024]{2,1,0:T(8,128)(2,1)}, bf16[128,1152]{1,0:T(8,128)(2,1)}, f32[8,128]{1,0:T(8,128)}) custom-call(bf16[1536,2048]{1,0:T(8,128)(2,1)} %x_ref.5, bf16[1536,512]{1,0:T(8,128)(2,1)} %bitcast.15, ...), custom_call_target="tpu_custom_call", output_to_operand_aliasing={{0}: (9, {}), {1}: (10, {}), {2}: (11, {})} | custom-call | flops 201326592 | bytes 6291456 | tf_op jit(solution)/shard_map/states/pallas_call | solution.py:249
  56.1 0.0 all-to-all-done.1
  56.2 0.0 copy-start.1
  56.2 0.7 copy-done.1
  56.9 2.8 %outputs.10.rest_0_ = bf16[128,1024]{1,0:T(8,128)(2,1)} custom-call(s32[1]{0:T(128)} %bitcast.where_ref.me_ref, bf16[1536,1024]{1,0:T(8,128)(2,1)} %get-tuple-element.39.x_ref, bf16[1536,256]{1,0:T(8,128)(2,1)} %get-tuple-element.40.maps_ref, bf16[1536,2048]{1,0:T(8,128)(2,1)} %gate_ref.19, bf16[1536,128]{1,0:T(8,128)(2,1)} %get-tuple-element.34.split_ref, ...), custom_call_target="tpu_custom_call" | custom-call | flops 100663296 | bytes 1048576 | tf_op jit(solution)/shard_map/outputs/pallas_call | solution.py:438
  59.7 0.0 copy-start.7
  59.7 3.9 %outputs.11.rest_0_ = bf16[256,1024]{1,0:T(8,128)(2,1)} custom-call(s32[1]{0:T(128)} %bitcast.where_ref.me_ref, bf16[1536,1024]{1,0:T(8,128)(2,1)} %get-tuple-element.39.x_ref, bf16[1536,256]{1,0:T(8,128)(2,1)} %get-tuple-element.40.maps_ref, bf16[1536,2048]{1,0:T(8,128)(2,1)} %gate_ref.19, bf16[1536,128]{1,0:T(8,128)(2,1)} %get-tuple-element.34.split_ref, ...), custom_call_target="tpu_custom_call" | custom-call | flops 201326592 | bytes 2097152 | tf_op jit(solution)/shard_map/outputs/pallas_call | solution.py:438
  63.6 0.0 copy-done.7
  63.6 11.5 %all_to_all.21.part_ref = bf16[8,16,1152]{2,1,0:T(8,128)(2,1)S(1)} all-to-all(bf16[8,16,1152]{2,1,0:T(8,128)(2,1)S(1)} %bitcast.37), channel_id=1, replica_groups=mesh['ctx'=8,'head'=4] {'ctx'}, dimensions={0} | all-to-all | bytes 589824 | tf_op jit(solution)/shard_map/all_to_all | solution.py:546
  75.1 0.9 scan_shards.3
  76.0 6.5 %all-to-all-start.3 = ((bf16[8,16,1024]{2,1,0:T(8,128)(2,1)}), bf16[8,16,1024]{2,1,0:T(8,128)(2,1)S(1)}, u32[]{:S(2)}, u32[]{:S(2)}) async-start(bf16[8,16,1024]{2,1,0:T(8,128)(2,1)} %scan_shards.3), calls=%async_computation.3 | async-start | bytes 524288 | tf_op jit(solution)/shard_map/all_to_all | solution.py:546
  82.6 0.0 collective-permute-start.6
  82.6 5.0 %outputs.12.rest_0_ = bf16[384,1024]{1,0:T(8,128)(2,1)} custom-call(s32[1]{0:T(128)} %bitcast.where_ref.me_ref, bf16[1536,1024]{1,0:T(8,128)(2,1)} %get-tuple-element.39.x_ref, bf16[1536,256]{1,0:T(8,128)(2,1)} %get-tuple-element.40.maps_ref, bf16[1536,2048]{1,0:T(8,128)(2,1)} %gate_ref.19, bf16[1536,128]{1,0:T(8,128)(2,1)} %get-tuple-element.34.split_ref, ...), custom_call_target="tpu_custom_call" | custom-call | flops 301989888 | bytes 3145728 | tf_op jit(solution)/shard_map/outputs/pallas_call | solution.py:438
  87.6 1.5 collective-permute-start.7
  89.1 5.0 %outputs.17 = bf16[384,1024]{1,0:T(8,128)(2,1)} custom-call(s32[1]{0:T(128)} %bitcast.where_ref.me_ref, bf16[1536,1024]{1,0:T(8,128)(2,1)} %get-tuple-element.39.x_ref, bf16[1536,256]{1,0:T(8,128)(2,1)} %get-tuple-element.40.maps_ref, bf16[1536,2048]{1,0:T(8,128)(2,1)} %gate_ref.19, bf16[1536,128]{1,0:T(8,128)(2,1)} %get-tuple-element.34.split_ref, ...), custom_call_target="tpu_custom_call" | custom-call | flops 301989888 | bytes 3145728 | tf_op jit(solution)/shard_map/outputs/pallas_call | solution.py:438
  94.1 0.3 collective-permute-start.8
  94.5 0.0 all-to-all-done.3
  94.5 0.7 copy-done
  95.2 2.8 %outputs.13.rest_0_ = bf16[128,1024]{1,0:T(8,128)(2,1)} custom-call(s32[1]{0:T(128)} %bitcast.where_ref.me_ref, bf16[1536,1024]{1,0:T(8,128)(2,1)} %get-tuple-element.32.x_ref, bf16[1536,256]{1,0:T(8,128)(2,1)} %get-tuple-element.33.maps_ref, bf16[1536,2048]{1,0:T(8,128)(2,1)} %gate_ref.19, bf16[1536,128]{1,0:T(8,128)(2,1)} %get-tuple-element.34.split_ref, ...), custom_call_target="tpu_custom_call" | custom-call | flops 100663296 | bytes 1048576 | tf_op jit(solution)/shard_map/outputs/pallas_call | solution.py:438
  98.0 3.8 %outputs.14.rest_0_ = bf16[256,1024]{1,0:T(8,128)(2,1)} custom-call(s32[1]{0:T(128)} %bitcast.where_ref.me_ref, bf16[1536,1024]{1,0:T(8,128)(2,1)} %get-tuple-element.32.x_ref, bf16[1536,256]{1,0:T(8,128)(2,1)} %get-tuple-element.33.maps_ref, bf16[1536,2048]{1,0:T(8,128)(2,1)} %gate_ref.19, bf16[1536,128]{1,0:T(8,128)(2,1)} %get-tuple-element.34.split_ref, ...), custom_call_target="tpu_custom_call" | custom-call | flops 201326592 | bytes 2097152 | tf_op jit(solution)/shard_map/outputs/pallas_call | solution.py:438
  101.9 3.8 %outputs.15.rest_0_ = bf16[256,1024]{1,0:T(8,128)(2,1)} custom-call(s32[1]{0:T(128)} %bitcast.where_ref.me_ref, bf16[1536,1024]{1,0:T(8,128)(2,1)} %get-tuple-element.32.x_ref, bf16[1536,256]{1,0:T(8,128)(2,1)} %get-tuple-element.33.maps_ref, bf16[1536,2048]{1,0:T(8,128)(2,1)} %gate_ref.19, bf16[1536,128]{1,0:T(8,128)(2,1)} %get-tuple-element.34.split_ref, ...), custom_call_target="tpu_custom_call" | custom-call | flops 201326592 | bytes 2097152 | tf_op jit(solution)/shard_map/outputs/pallas_call | solution.py:438
  105.7 2.8 %outputs.16.rest_0_ = bf16[128,1024]{1,0:T(8,128)(2,1)} custom-call(s32[1]{0:T(128)} %bitcast.where_ref.me_ref, bf16[1536,1024]{1,0:T(8,128)(2,1)} %get-tuple-element.32.x_ref, bf16[1536,256]{1,0:T(8,128)(2,1)} %get-tuple-element.33.maps_ref, bf16[1536,2048]{1,0:T(8,128)(2,1)} %gate_ref.19, bf16[1536,128]{1,0:T(8,128)(2,1)} %get-tuple-element.34.split_ref, ...), custom_call_target="tpu_custom_call" | custom-call | flops 100663296 | bytes 1048576 | tf_op jit(solution)/shard_map/outputs/pallas_call | solution.py:438
  108.5 5.0 %outputs.18.rest_1_ = bf16[384,8192]{1,0:T(8,128)(2,1)} custom-call(s32[1]{0:T(128)} %bitcast.where_ref.me_ref, bf16[1536,1024]{1,0:T(8,128)(2,1)} %get-tuple-element.39.x_ref, bf16[1536,256]{1,0:T(8,128)(2,1)} %get-tuple-element.40.maps_ref, bf16[1536,2048]{1,0:T(8,128)(2,1)} %gate_ref.19, bf16[1536,128]{1,0:T(8,128)(2,1)} %get-tuple-element.34.split_ref, ...), custom_call_target="tpu_custom_call" | custom-call | flops 301989888 | bytes 3145728 | tf_op jit(solution)/shard_map/outputs/pallas_call | solution.py:438
  113.6 0.0 copy-start.4
  113.6 0.0 copy-start.3
  113.6 0.0 copy-start.5
  113.6 0.0 copy-start.2
  113.6 8.4 %outputs.19 = (bf16[384,1024]{1,0:T(8,128)(2,1)}, bf16[384,8192]{1,0:T(8,128)(2,1)}) custom-call(s32[1]{0:T(128)} %bitcast.where_ref.me_ref, bf16[1536,1024]{1,0:T(8,128)(2,1)} %get-tuple-element.32.x_ref, bf16[1536,256]{1,0:T(8,128)(2,1)} %get-tuple-element.33.maps_ref, bf16[1536,2048]{1,0:T(8,128)(2,1)} %gate_ref.19, ...), custom_call_target="tpu_custom_call", output_to_operand_aliasing={{1}: (14, {})} | custom-call | flops 603979776 | bytes 6291456 | tf_op jit(solution)/shard_map/outputs/pallas_call | solution.py:438
  122.0 0.2 collective-permute-start.9
  122.3 0.0 copy-done.6
  122.3 1.5 collective-permute-start.5
  123.7 6.6 %collective-permute-done.5.refs_0_ = bf16[128,1024]{1,0:T(8,128)(2,1)S(1)} collective-permute-done((bf16[128,1024]{1,0:T(8,128)(2,1)S(1)}, bf16[128,1024]{1,0:T(8,128)(2,1)S(1)}, u32[]{:S(2)}, u32[]{:S(2)}) %collective-permute-start.5) | collective-permute-done | bytes 262176 | tf_op jit(solution)/shard_map/ppermute | solution.py:555
  130.4 0.0 copy-done.4
  130.4 1.4 collective-permute-start.3
  131.8 0.0 collective-permute-done.6.refs_1_
  131.8 0.0 copy-done.3
  131.8 0.6 collective-permute-start.4
  132.4 0.0 collective-permute-done.7.refs_2_
  132.4 0.0 copy-done.5
  132.4 0.8 collective-permute-start.2
  133.2 0.0 collective-permute-done.8.refs_3_
  133.2 0.0 copy-done.2
  133.2 0.7 collective-permute-start.1
  133.9 0.0 collective-permute-done.9.refs_4_
  133.9 2.0 %place.3.refs_3_ = bf16[384,8192]{1,0:T(8,128)(2,1)} custom-call(s32[1]{0:T(128)} %bitcast.where_ref.me_ref, bf16[128,1024]{1,0:T(8,128)(2,1)S(1)} %collective-permute-done.5.refs_0_, bf16[256,1024]{1,0:T(8,128)(2,1)S(1)} %collective-permute-done.6.refs_1_, bf16[384,1024]{1,0:T(8,128)(2,1)S(1)} %collective-permute-done.7.refs_2_, ...), custom_call_target="tpu_custom_call", output_to_operand_aliasing={{}: (6, {})} | custom-call | bytes 6291456 | tf_op jit(solution)/shard_map/place/pallas_call | solution.py:486
  135.9 25.1 %collective-permute-done.2.refs_0_ = bf16[128,1024]{1,0:T(8,128)(2,1)S(1)} collective-permute-done((bf16[128,1024]{1,0:T(8,128)(2,1)S(1)}, bf16[128,1024]{1,0:T(8,128)(2,1)S(1)}, u32[]{:S(2)}, u32[]{:S(2)}) %collective-permute-start.2) | collective-permute-done | bytes 262176 | tf_op jit(solution)/shard_map/ppermute | solution.py:555
  160.9 0.0 collective-permute-done.3.refs_1_
  160.9 0.0 collective-permute-done.4.refs_2_
  160.9 1.2 place.4.refs_1_
  162.1 4.9 %collective-permute-done.1.refs_0_ = bf16[128,1024]{1,0:T(8,128)(2,1)S(1)} collective-permute-done((bf16[128,1024]{1,0:T(8,128)(2,1)S(1)}, bf16[128,1024]{1,0:T(8,128)(2,1)S(1)}, u32[]{:S(2)}, u32[]{:S(2)}) %collective-permute-start.1) | collective-permute-done | bytes 262176 | tf_op jit(solution)/shard_map/ppermute | solution.py:555
  167.1 0.7 place.5
  (4 shorter events, 0.0 us)
Async XLA Ops:
  1.5 7.5 %collective-permute-start = (bf16[8,2560]{1,0:T(8,128)(2,1)S(1)}, bf16[8,2560]{1,0:T(8,128)(2,1)S(1)}, u32[]{:S(2)}, u32[]{:S(2)}) collective-permute-start(bf16[8,2560]{1,0:T(8,128)(2,1)S(1)} %pad_maximum_fusion), channel_id=1, source_target_pairs={{0,4},{4,8},{8,12},{12,16},{16,20},{20,24},{24,28},{1,5},{5,9},{9,... | collective-permute-start | bytes 122888 | tf_op jit(solution)/shard_map/ppermute | solution.py:529
  9.0 0.6 copy-start.8
  35.4 20.8 %all-to-all-start.1 = ((bf16[8,16,1024]{2,1,0:T(8,128)(2,1)}), bf16[8,16,1024]{2,1,0:T(8,128)(2,1)S(1)}, u32[]{:S(2)}, u32[]{:S(2)}) async-start(bf16[8,16,1024]{2,1,0:T(8,128)(2,1)} %scan_shards.2), calls=%async_computation.1 | async-start | bytes 524288 | tf_op jit(solution)/shard_map/all_to_all | solution.py:546
  56.2 0.7 copy-start.1
  59.7 3.9 %copy-start.7 = (bf16[128,1152]{1,0:T(8,128)(2,1)S(1)}, bf16[128,1152]{1,0:T(8,128)(2,1)}, u32[]{:S(2)}) copy-start(bf16[128,1152]{1,0:T(8,128)(2,1)} %get-tuple-element.38) | copy-start | bytes 884740
  76.0 18.4 %all-to-all-start.3 = ((bf16[8,16,1024]{2,1,0:T(8,128)(2,1)}), bf16[8,16,1024]{2,1,0:T(8,128)(2,1)S(1)}, u32[]{:S(2)}, u32[]{:S(2)}) async-start(bf16[8,16,1024]{2,1,0:T(8,128)(2,1)} %scan_shards.3), calls=%async_computation.3 | async-start | bytes 524288 | tf_op jit(solution)/shard_map/all_to_all | solution.py:546
  82.6 49.2 %collective-permute-start.6 = (bf16[256,1024]{1,0:T(8,128)(2,1)}, bf16[256,1024]{1,0:T(8,128)(2,1)S(1)}, u32[]{:S(2)}, u32[]{:S(2)}) collective-permute-start(bf16[256,1024]{1,0:T(8,128)(2,1)} %outputs.11.rest_0_), channel_id=1, source_target_pairs={{0,3},{1,2},{2,1},{3,0},{4,7},{5,6},{6,5},{7,4},{8,11},{9,10},{10,... | collective-permute-start | bytes 1572872 | tf_op jit(solution)/shard_map/ppermute | solution.py:555
  87.6 44.8 %collective-permute-start.7 = (bf16[384,1024]{1,0:T(8,128)(2,1)}, bf16[384,1024]{1,0:T(8,128)(2,1)S(1)}, u32[]{:S(2)}, u32[]{:S(2)}) collective-permute-start(bf16[384,1024]{1,0:T(8,128)(2,1)} %outputs.12.rest_0_), channel_id=1, source_target_pairs={{0,2},{1,3},{2,0},{3,1},{4,6},{5,7},{6,4},{7,5},{8,10},{9,11},{10,... | collective-permute-start | bytes 2359304 | tf_op jit(solution)/shard_map/ppermute | solution.py:555
  94.1 39.1 %collective-permute-start.8 = (bf16[384,1024]{1,0:T(8,128)(2,1)}, bf16[384,1024]{1,0:T(8,128)(2,1)S(1)}, u32[]{:S(2)}, u32[]{:S(2)}) collective-permute-start(bf16[384,1024]{1,0:T(8,128)(2,1)} %outputs.17), channel_id=1, source_target_pairs={{0,1},{1,0},{2,3},{3,2},{4,5},{5,4},{6,7},{7,6},{8,9},{9,8},{10,11... | collective-permute-start | bytes 2359304 | tf_op jit(solution)/shard_map/ppermute | solution.py:555
  94.5 0.7 copy-start
  113.6 8.7 %copy-start.6 = (bf16[128,1024]{1,0:T(8,128)(2,1)S(1)}, bf16[128,1024]{1,0:T(8,128)(2,1)}, u32[]{:S(2)}) copy-start(bf16[128,1024]{1,0:T(8,128)(2,1)} %outputs.10.rest_0_) | copy-start | bytes 786436
  113.6 16.8 %copy-start.4 = (bf16[256,1024]{1,0:T(8,128)(2,1)S(1)}, bf16[256,1024]{1,0:T(8,128)(2,1)}, u32[]{:S(2)}) copy-start(bf16[256,1024]{1,0:T(8,128)(2,1)} %outputs.14.rest_0_) | copy-start | bytes 1572868
  113.6 18.2 %copy-start.3 = (bf16[256,1024]{1,0:T(8,128)(2,1)S(1)}, bf16[256,1024]{1,0:T(8,128)(2,1)}, u32[]{:S(2)}) copy-start(bf16[256,1024]{1,0:T(8,128)(2,1)} %outputs.15.rest_0_) | copy-start | bytes 1572868
  113.6 18.7 %copy-start.5 = (bf16[128,1024]{1,0:T(8,128)(2,1)S(1)}, bf16[128,1024]{1,0:T(8,128)(2,1)}, u32[]{:S(2)}) copy-start(bf16[128,1024]{1,0:T(8,128)(2,1)} %outputs.13.rest_0_) | copy-start | bytes 786436
  113.6 19.6 %copy-start.2 = (bf16[128,1024]{1,0:T(8,128)(2,1)S(1)}, bf16[128,1024]{1,0:T(8,128)(2,1)}, u32[]{:S(2)}) copy-start(bf16[128,1024]{1,0:T(8,128)(2,1)} %outputs.16.rest_0_) | copy-start | bytes 786436
  122.0 11.8 %collective-permute-start.9 = (bf16[384,1024]{1,0:T(8,128)(2,1)}, bf16[384,1024]{1,0:T(8,128)(2,1)S(1)}, u32[]{:S(2)}, u32[]{:S(2)}) collective-permute-start(bf16[384,1024]{1,0:T(8,128)(2,1)} %get-tuple-element.45), channel_id=1, source_target_pairs={{0,1},{1,0},{2,3},{3,2},{4,5},{5,4},{6,7},{7,6},{8,9},{9,8},{10,11... | collective-permute-start | bytes 2359304 | tf_op jit(solution)/shard_map/ppermute | solution.py:555
  122.3 8.1 %collective-permute-start.5 = (bf16[128,1024]{1,0:T(8,128)(2,1)S(1)}, bf16[128,1024]{1,0:T(8,128)(2,1)S(1)}, u32[]{:S(2)}, u32[]{:S(2)}) collective-permute-start(bf16[128,1024]{1,0:T(8,128)(2,1)S(1)} %copy-done.6), channel_id=1, source_target_pairs={{0,3},{1,2},{2,1},{3,0},{4,7},{5,6},{6,5},{7,4},{8,11},{9,10},{10,... | collective-permute-start | bytes 786440 | tf_op jit(solution)/shard_map/ppermute | solution.py:555
  130.4 30.6 %collective-permute-start.3 = (bf16[256,1024]{1,0:T(8,128)(2,1)S(1)}, bf16[256,1024]{1,0:T(8,128)(2,1)S(1)}, u32[]{:S(2)}, u32[]{:S(2)}) collective-permute-start(bf16[256,1024]{1,0:T(8,128)(2,1)S(1)} %copy-done.4), channel_id=1, source_target_pairs={{0,3},{1,2},{2,1},{3,0},{4,7},{5,6},{6,5},{7,4},{8,11},{9,10},{10,... | collective-permute-start | bytes 1572872 | tf_op jit(solution)/shard_map/ppermute | solution.py:555
  131.8 29.2 %collective-permute-start.4 = (bf16[256,1024]{1,0:T(8,128)(2,1)S(1)}, bf16[256,1024]{1,0:T(8,128)(2,1)S(1)}, u32[]{:S(2)}, u32[]{:S(2)}) collective-permute-start(bf16[256,1024]{1,0:T(8,128)(2,1)S(1)} %copy-done.3), channel_id=1, source_target_pairs={{0,2},{1,3},{2,0},{3,1},{4,6},{5,7},{6,4},{7,5},{8,10},{9,11},{10,... | collective-permute-start | bytes 1572872 | tf_op jit(solution)/shard_map/ppermute | solution.py:555
  132.4 28.6 %collective-permute-start.2 = (bf16[128,1024]{1,0:T(8,128)(2,1)S(1)}, bf16[128,1024]{1,0:T(8,128)(2,1)S(1)}, u32[]{:S(2)}, u32[]{:S(2)}) collective-permute-start(bf16[128,1024]{1,0:T(8,128)(2,1)S(1)} %copy-done.5), channel_id=1, source_target_pairs={{0,3},{1,2},{2,1},{3,0},{4,7},{5,6},{6,5},{7,4},{8,11},{9,10},{10,... | collective-permute-start | bytes 786440 | tf_op jit(solution)/shard_map/ppermute | solution.py:555
  133.2 33.9 %collective-permute-start.1 = (bf16[128,1024]{1,0:T(8,128)(2,1)S(1)}, bf16[128,1024]{1,0:T(8,128)(2,1)S(1)}, u32[]{:S(2)}, u32[]{:S(2)}) collective-permute-start(bf16[128,1024]{1,0:T(8,128)(2,1)S(1)} %copy-done.2), channel_id=1, source_target_pairs={{0,2},{1,3},{2,0},{3,1},{4,6},{5,7},{6,4},{7,5},{8,10},{9,11},{10,... | collective-permute-start | bytes 786440 | tf_op jit(solution)/shard_map/ppermute | solution.py:555

commit v2 on v1

--- a/solution.py
+++ b/solution.py
@@ -69,7 +69,7 @@
         cum = summed[k * heads : (k + 1) * heads]
         final = cum[:, q - 1 : q]
         rel = cum - shift[:, k * q : (k + 1) * q]
-        held[k] = rel
+        held[k, :heads] = rel
         even = held[k, pl.ds(0, heads // 2, stride=2), :]
         odd = held[k, pl.ds(1, heads // 2, stride=2), :]
         for j in range(q // SUB):
@@ -114,7 +114,7 @@
             jax.ShapeDtypeStruct((blocks + 1, 1, heads * HEAD_DIM), F32),
             jax.ShapeDtypeStruct((1, heads * HEAD_DIM), F32),
         ),
-        scratch_shapes=[pltpu.VMEM((blocks, heads, q), F32)],
+        scratch_shapes=[pltpu.VMEM((blocks, heads + 8, q), F32)],
         compiler_params=pltpu.CompilerParams(vmem_limit_bytes=VMEM_LIMIT),
         cost_estimate=cost(rows * q * heads * 12, rows * heads * 16, rows * heads * 4),
         name="prep",
@@ -561,7 +561,7 @@
     for group in range(groups):
         payload = payloads[group]
         if group > 0:
-            payload, _ = lax.optimization_barrier((payload, tokens[1]))
+            payload, _ = lax.optimization_barrier((payload, tokens[0]))
         part = exchange(payload)
         part = scan_shards(part)
         entering.append(exchange(part).reshape(STATE, width))
@@ -592,6 +592,8 @@
 
 
 def sends(group, groups, far, peers, blocks):
+    if blocks > 1 and groups > 1 and group == 0 and far == peers - 1:
+        return [(0, blocks - 1), (blocks - 1, blocks)]
     if blocks > 1 and far == peers - 1:
         return [(0, 1), (1, blocks)]
     if blocks > 1 and group == groups - 1 and far == 2:

time: 171 us -> 171 us (level)
  transfers between devices with their start and end apart: 12 -> 12, of which waited for: 3 -> 3; matrix products, arithmetic and copies ran while one was open for 2% -> 2% of each run, Pallas kernels for 34% -> 36%
where the time goes in v2:
time: 171 us; the launch traced here: 168 us
  Pallas kernels  77.6 us (45%)
  waiting for transfers between devices  36.7 us (21%)
  blocking collectives  25.7 us (15%)
  starting transfers between devices  21.4 us (13%)
  local copies, waits for them, and re-layouts  6.37 us (4%)
    pallas_call x10, Pallas kernels, outputs(): pl.pallas_call(functools.partial(outputs_kernel, group, blocks if home el...  43.6 us
    ppermute x9, waiting for transfers between devices, send(): return lax.ppermute(block, 'head', [(i, i ^ far) for i in range(peers)])  36.7 us
    all_to_all x2, blocking collectives, exchange(): return lax.all_to_all(payload, 'ctx', 0, 0, tiled=True)  25.7 us
    pallas_call x3, Pallas kernels, states(): pl.pallas_call(functools.partial(states_kernel, group, groups, pieces, q,...  24.9 us
    all_to_all x2, starting transfers between devices, exchange(): return lax.all_to_all(payload, 'ctx', 0, 0, tiled=True)  13 us
    ppermute x9, starting transfers between devices, send(): return lax.ppermute(block, 'head', [(i, i ^ far) for i in range(peers)])  7.05 us
    unnamed x21, local copies, waits for them, and re-layouts  5.61 us
    pallas_call x3, Pallas kernels, place(): pl.pallas_call(functools.partial(place_kernel, places, width), in_specs=[...  3.89 us
  transfers between devices with their start and end apart: 12, of which 3 were waited for; matrix products, arithmetic and copies ran while one was open for 2% of the time, Pallas kernels for 36%

profile of v2, /device:TPU:26, one launch (start us, length us, event | category | flops | bytes accessed | tf_op | source)
XLA Modules:
  0.0 168.0 jit_solution(7002497145512929126)
XLA Ops:
  0.0 0.7 slice_bitcast_fusion
  0.7 0.8 slice.9
  1.5 1.3 collective-permute-start
  2.8 2.9 %copy.31 = bf16[192,8,2,256]{3,1,2,0:T(8,128)(2,1)} copy(bf16[192,8,2,256]{3,2,1,0:T(2,128)(2,1)} %bitcast.26) | data formatting | bytes 3145728
  5.6 3.4 %prep.1 = (bf16[1536,128]{1,0:T(8,128)(2,1)}, bf16[1536,128]{1,0:T(8,128)(2,1)}, f32[12,2,16,128]{3,2,1,0:T(8,128)}, f32[13,32]{1,0:T(8,128)}, f32[13,1,2048]{2,1,0:T(1,128)}, /*index=5*/f32[1,2048]{1,0:T(1,128)}) custom-call(f32[32,1536]{1,0:T(8,128)} %bitcast.39, f32[2,32]{1,0:T(2,128)} %rates_ref.1, f32[1,32]{1,0:T(1,128)} %bitcast.41, ...), custom_call_target="tpu_custom_call" | custom-call | flops 75497472 | bytes 786432 | tf_op jit(solution)/shard_map/prep/pallas_call | solution.py:107
  9.0 0.0 collective-permute-done.halo_ref
  9.0 0.0 copy-start.8
  9.0 0.6 copy-done.8
  9.6 10.7 %states.5 = (bf16[1536,1024]{1,0:T(8,128)(2,1)}, bf16[1536,256]{1,0:T(8,128)(2,1)}, bf16[12,128,1024]{2,1,0:T(8,128)(2,1)}, bf16[128,1152]{1,0:T(8,128)(2,1)}, f32[8,128]{1,0:T(8,128)}) custom-call(bf16[1536,2048]{1,0:T(8,128)(2,1)} %x_ref.5, bf16[1536,512]{1,0:T(8,128)(2,1)} %bitcast.13, bf16[1536,128]{1,0:T(8,128)(2,1)} %get-tuple-element.26.spread_ref, ...), custom_call_target="tpu_custom_call" | custom-call | flops 402653184 | bytes 12582912 | tf_op jit(solution)/shard_map/states/pallas_call | solution.py:249
  20.3 14.1 %all_to_all.20.part_ref = bf16[8,16,1152]{2,1,0:T(8,128)(2,1)S(1)} all-to-all(bf16[8,16,1152]{2,1,0:T(8,128)(2,1)} %bitcast.38), channel_id=1, replica_groups=mesh['ctx'=8,'head'=4] {'ctx'}, dimensions={0} | all-to-all | bytes 589824 | tf_op jit(solution)/shard_map/all_to_all | solution.py:546
  34.4 0.9 scan_shards.2
  35.4 6.5 %all-to-all-start.1 = ((bf16[8,16,1024]{2,1,0:T(8,128)(2,1)}), bf16[8,16,1024]{2,1,0:T(8,128)(2,1)S(1)}, u32[]{:S(2)}, u32[]{:S(2)}) async-start(bf16[8,16,1024]{2,1,0:T(8,128)(2,1)} %scan_shards.2), calls=%async_computation.1 | async-start | bytes 524288 | tf_op jit(solution)/shard_map/all_to_all | solution.py:546
  41.9 7.0 %states.3 = (bf16[1536,1024]{1,0:T(8,128)(2,1)}, bf16[1536,256]{1,0:T(8,128)(2,1)}, bf16[12,128,1024]{2,1,0:T(8,128)(2,1)}, bf16[8,128]{1,0:T(8,128)(2,1)}, f32[144,1024]{1,0:T(8,128)}) custom-call(bf16[1536,2048]{1,0:T(8,128)(2,1)} %x_ref.5, bf16[1536,512]{1,0:T(8,128)(2,1)} %bitcast.14, bf16[1536,128]{1,0:T(8,128)(2,1)} %get-tuple-element.26.spread_ref, ...), custom_call_target="tpu_custom_call" | custom-call | flops 201326592 | bytes 6291456 | tf_op jit(solution)/shard_map/states/pallas_call | solution.py:249
  48.9 7.2 %states.4 = (bf16[1536,1024]{1,0:T(8,128)(2,1)}, bf16[1536,256]{1,0:T(8,128)(2,1)}, bf16[12,128,1024]{2,1,0:T(8,128)(2,1)}, bf16[128,1152]{1,0:T(8,128)(2,1)}, f32[8,128]{1,0:T(8,128)}) custom-call(bf16[1536,2048]{1,0:T(8,128)(2,1)} %x_ref.5, bf16[1536,512]{1,0:T(8,128)(2,1)} %bitcast.15, ...), custom_call_target="tpu_custom_call", output_to_operand_aliasing={{0}: (9, {}), {1}: (10, {}), {2}: (11, {})} | custom-call | flops 201326592 | bytes 6291456 | tf_op jit(solution)/shard_map/states/pallas_call | solution.py:249
  56.1 0.0 all-to-all-done.1
  56.2 0.0 copy-start.1
  56.2 0.7 copy-done.1
  56.9 0.0 copy-start.7
  56.9 3.9 %outputs.10.rest_0_ = bf16[256,1024]{1,0:T(8,128)(2,1)} custom-call(s32[1]{0:T(128)} %bitcast.where_ref.me_ref, bf16[1536,1024]{1,0:T(8,128)(2,1)} %get-tuple-element.39.x_ref, bf16[1536,256]{1,0:T(8,128)(2,1)} %get-tuple-element.40.maps_ref, bf16[1536,2048]{1,0:T(8,128)(2,1)} %gate_ref.19, bf16[1536,128]{1,0:T(8,128)(2,1)} %get-tuple-element.34.split_ref, ...), custom_call_target="tpu_custom_call" | custom-call | flops 201326592 | bytes 2097152 | tf_op jit(solution)/shard_map/outputs/pallas_call | solution.py:438
  60.7 0.0 copy-done.7
  60.7 11.5 %all_to_all.21.part_ref = bf16[8,16,1152]{2,1,0:T(8,128)(2,1)S(1)} all-to-all(bf16[8,16,1152]{2,1,0:T(8,128)(2,1)S(1)} %bitcast.37), channel_id=1, replica_groups=mesh['ctx'=8,'head'=4] {'ctx'}, dimensions={0} | all-to-all | bytes 589824 | tf_op jit(solution)/shard_map/all_to_all | solution.py:546
  72.3 0.9 scan_shards.3
  73.2 6.5 %all-to-all-start.3 = ((bf16[8,16,1024]{2,1,0:T(8,128)(2,1)}), bf16[8,16,1024]{2,1,0:T(8,128)(2,1)S(1)}, u32[]{:S(2)}, u32[]{:S(2)}) async-start(bf16[8,16,1024]{2,1,0:T(8,128)(2,1)} %scan_shards.3), calls=%async_computation.3 | async-start | bytes 524288 | tf_op jit(solution)/shard_map/all_to_all | solution.py:546
  79.7 0.0 collective-permute-start.5
  79.7 2.8 %outputs.11.rest_0_ = bf16[128,1024]{1,0:T(8,128)(2,1)} custom-call(s32[1]{0:T(128)} %bitcast.where_ref.me_ref, bf16[1536,1024]{1,0:T(8,128)(2,1)} %get-tuple-element.39.x_ref, bf16[1536,256]{1,0:T(8,128)(2,1)} %get-tuple-element.40.maps_ref, bf16[1536,2048]{1,0:T(8,128)(2,1)} %gate_ref.19, bf16[1536,128]{1,0:T(8,128)(2,1)} %get-tuple-element.34.split_ref, ...), custom_call_target="tpu_custom_call" | custom-call | flops 100663296 | bytes 1048576 | tf_op jit(solution)/shard_map/outputs/pallas_call | solution.py:438
  82.6 5.0 %outputs.12.rest_0_ = bf16[384,1024]{1,0:T(8,128)(2,1)} custom-call(s32[1]{0:T(128)} %bitcast.where_ref.me_ref, bf16[1536,1024]{1,0:T(8,128)(2,1)} %get-tuple-element.39.x_ref, bf16[1536,256]{1,0:T(8,128)(2,1)} %get-tuple-element.40.maps_ref, bf16[1536,2048]{1,0:T(8,128)(2,1)} %gate_ref.19, bf16[1536,128]{1,0:T(8,128)(2,1)} %get-tuple-element.34.split_ref, ...), custom_call_target="tpu_custom_call" | custom-call | flops 301989888 | bytes 3145728 | tf_op jit(solution)/shard_map/outputs/pallas_call | solution.py:438
  87.6 1.5 collective-permute-start.7
  89.1 5.0 %outputs.17 = bf16[384,1024]{1,0:T(8,128)(2,1)} custom-call(s32[1]{0:T(128)} %bitcast.where_ref.me_ref, bf16[1536,1024]{1,0:T(8,128)(2,1)} %get-tuple-element.39.x_ref, bf16[1536,256]{1,0:T(8,128)(2,1)} %get-tuple-element.40.maps_ref, bf16[1536,2048]{1,0:T(8,128)(2,1)} %gate_ref.19, bf16[1536,128]{1,0:T(8,128)(2,1)} %get-tuple-element.34.split_ref, ...), custom_call_target="tpu_custom_call" | custom-call | flops 301989888 | bytes 3145728 | tf_op jit(solution)/shard_map/outputs/pallas_call | solution.py:438
  94.1 0.3 collective-permute-start.8
  94.5 0.0 all-to-all-done.3
  94.5 0.7 copy-done
  95.2 2.8 %outputs.13.rest_0_ = bf16[128,1024]{1,0:T(8,128)(2,1)} custom-call(s32[1]{0:T(128)} %bitcast.where_ref.me_ref, bf16[1536,1024]{1,0:T(8,128)(2,1)} %get-tuple-element.32.x_ref, bf16[1536,256]{1,0:T(8,128)(2,1)} %get-tuple-element.33.maps_ref, bf16[1536,2048]{1,0:T(8,128)(2,1)} %gate_ref.19, bf16[1536,128]{1,0:T(8,128)(2,1)} %get-tuple-element.34.split_ref, ...), custom_call_target="tpu_custom_call" | custom-call | flops 100663296 | bytes 1048576 | tf_op jit(solution)/shard_map/outputs/pallas_call | solution.py:438
  98.0 3.8 %outputs.14.rest_0_ = bf16[256,1024]{1,0:T(8,128)(2,1)} custom-call(s32[1]{0:T(128)} %bitcast.where_ref.me_ref, bf16[1536,1024]{1,0:T(8,128)(2,1)} %get-tuple-element.32.x_ref, bf16[1536,256]{1,0:T(8,128)(2,1)} %get-tuple-element.33.maps_ref, bf16[1536,2048]{1,0:T(8,128)(2,1)} %gate_ref.19, bf16[1536,128]{1,0:T(8,128)(2,1)} %get-tuple-element.34.split_ref, ...), custom_call_target="tpu_custom_call" | custom-call | flops 201326592 | bytes 2097152 | tf_op jit(solution)/shard_map/outputs/pallas_call | solution.py:438
  101.9 3.8 %outputs.15.rest_0_ = bf16[256,1024]{1,0:T(8,128)(2,1)} custom-call(s32[1]{0:T(128)} %bitcast.where_ref.me_ref, bf16[1536,1024]{1,0:T(8,128)(2,1)} %get-tuple-element.32.x_ref, bf16[1536,256]{1,0:T(8,128)(2,1)} %get-tuple-element.33.maps_ref, bf16[1536,2048]{1,0:T(8,128)(2,1)} %gate_ref.19, bf16[1536,128]{1,0:T(8,128)(2,1)} %get-tuple-element.34.split_ref, ...), custom_call_target="tpu_custom_call" | custom-call | flops 201326592 | bytes 2097152 | tf_op jit(solution)/shard_map/outputs/pallas_call | solution.py:438
  105.7 2.8 %outputs.16.rest_0_ = bf16[128,1024]{1,0:T(8,128)(2,1)} custom-call(s32[1]{0:T(128)} %bitcast.where_ref.me_ref, bf16[1536,1024]{1,0:T(8,128)(2,1)} %get-tuple-element.32.x_ref, bf16[1536,256]{1,0:T(8,128)(2,1)} %get-tuple-element.33.maps_ref, bf16[1536,2048]{1,0:T(8,128)(2,1)} %gate_ref.19, bf16[1536,128]{1,0:T(8,128)(2,1)} %get-tuple-element.34.split_ref, ...), custom_call_target="tpu_custom_call" | custom-call | flops 100663296 | bytes 1048576 | tf_op jit(solution)/shard_map/outputs/pallas_call | solution.py:438
  108.6 5.0 %outputs.18.rest_1_ = bf16[384,8192]{1,0:T(8,128)(2,1)} custom-call(s32[1]{0:T(128)} %bitcast.where_ref.me_ref, bf16[1536,1024]{1,0:T(8,128)(2,1)} %get-tuple-element.39.x_ref, bf16[1536,256]{1,0:T(8,128)(2,1)} %get-tuple-element.40.maps_ref, bf16[1536,2048]{1,0:T(8,128)(2,1)} %gate_ref.19, bf16[1536,128]{1,0:T(8,128)(2,1)} %get-tuple-element.34.split_ref, ...), custom_call_target="tpu_custom_call" | custom-call | flops 301989888 | bytes 3145728 | tf_op jit(solution)/shard_map/outputs/pallas_call | solution.py:438
  113.6 0.0 copy-start.4
  113.6 0.0 copy-start.3
  113.6 0.0 copy-start.5
  113.6 0.0 copy-start.2
  113.6 8.4 %outputs.19 = (bf16[384,1024]{1,0:T(8,128)(2,1)}, bf16[384,8192]{1,0:T(8,128)(2,1)}) custom-call(s32[1]{0:T(128)} %bitcast.where_ref.me_ref, bf16[1536,1024]{1,0:T(8,128)(2,1)} %get-tuple-element.32.x_ref, bf16[1536,256]{1,0:T(8,128)(2,1)} %get-tuple-element.33.maps_ref, bf16[1536,2048]{1,0:T(8,128)(2,1)} %gate_ref.19, ...), custom_call_target="tpu_custom_call", output_to_operand_aliasing={{1}: (14, {})} | custom-call | flops 603979776 | bytes 6291456 | tf_op jit(solution)/shard_map/outputs/pallas_call | solution.py:438
  122.1 0.2 collective-permute-start.9
  122.3 0.0 copy-done.6
  122.3 1.5 collective-permute-start.6
  123.7 6.6 %collective-permute-done.6.refs_1_ = bf16[128,1024]{1,0:T(8,128)(2,1)S(1)} collective-permute-done((bf16[128,1024]{1,0:T(8,128)(2,1)S(1)}, bf16[128,1024]{1,0:T(8,128)(2,1)S(1)}, u32[]{:S(2)}, u32[]{:S(2)}) %collective-permute-start.6) | collective-permute-done | bytes 262176 | tf_op jit(solution)/shard_map/ppermute | solution.py:555
  130.4 0.0 copy-done.4
  130.4 1.4 collective-permute-start.3
  131.8 0.0 collective-permute-done.5.refs_0_
  131.8 0.0 copy-done.3
  131.8 0.6 collective-permute-start.4
  132.4 0.0 collective-permute-done.7.refs_2_
  132.4 0.0 copy-done.5
  132.4 0.8 collective-permute-start.2
  133.2 0.0 collective-permute-done.8.refs_3_
  133.2 0.0 copy-done.2
  133.2 0.7 collective-permute-start.1
  133.9 0.0 collective-permute-done.9.refs_4_
  133.9 2.0 %place.3.refs_3_ = bf16[384,8192]{1,0:T(8,128)(2,1)} custom-call(s32[1]{0:T(128)} %bitcast.where_ref.me_ref, bf16[256,1024]{1,0:T(8,128)(2,1)S(1)} %collective-permute-done.5.refs_0_, bf16[128,1024]{1,0:T(8,128)(2,1)S(1)} %collective-permute-done.6.refs_1_, bf16[384,1024]{1,0:T(8,128)(2,1)S(1)} %collective-permute-done.7.refs_2_, ...), custom_call_target="tpu_custom_call", output_to_operand_aliasing={{}: (6, {})} | custom-call | bytes 6291456 | tf_op jit(solution)/shard_map/place/pallas_call | solution.py:486
  135.9 25.1 %collective-permute-done.2.refs_0_ = bf16[128,1024]{1,0:T(8,128)(2,1)S(1)} collective-permute-done((bf16[128,1024]{1,0:T(8,128)(2,1)S(1)}, bf16[128,1024]{1,0:T(8,128)(2,1)S(1)}, u32[]{:S(2)}, u32[]{:S(2)}) %collective-permute-start.2) | collective-permute-done | bytes 262176 | tf_op jit(solution)/shard_map/ppermute | solution.py:555
  160.9 0.0 collective-permute-done.3.refs_1_
  160.9 0.0 collective-permute-done.4.refs_2_
  160.9 1.2 place.4.refs_1_
  162.2 4.9 %collective-permute-done.1.refs_0_ = bf16[128,1024]{1,0:T(8,128)(2,1)S(1)} collective-permute-done((bf16[128,1024]{1,0:T(8,128)(2,1)S(1)}, bf16[128,1024]{1,0:T(8,128)(2,1)S(1)}, u32[]{:S(2)}, u32[]{:S(2)}) %collective-permute-start.1) | collective-permute-done | bytes 262176 | tf_op jit(solution)/shard_map/ppermute | solution.py:555
  167.1 0.7 place.5
  (4 shorter events, 0.0 us)
Async XLA Ops:
  1.5 7.5 %collective-permute-start = (bf16[8,2560]{1,0:T(8,128)(2,1)S(1)}, bf16[8,2560]{1,0:T(8,128)(2,1)S(1)}, u32[]{:S(2)}, u32[]{:S(2)}) collective-permute-start(bf16[8,2560]{1,0:T(8,128)(2,1)S(1)} %pad_maximum_fusion), channel_id=1, source_target_pairs={{0,4},{4,8},{8,12},{12,16},{16,20},{20,24},{24,28},{1,5},{5,9},{9,... | collective-permute-start | bytes 122888 | tf_op jit(solution)/shard_map/ppermute | solution.py:529
  9.0 0.6 copy-start.8
  35.4 20.8 %all-to-all-start.1 = ((bf16[8,16,1024]{2,1,0:T(8,128)(2,1)}), bf16[8,16,1024]{2,1,0:T(8,128)(2,1)S(1)}, u32[]{:S(2)}, u32[]{:S(2)}) async-start(bf16[8,16,1024]{2,1,0:T(8,128)(2,1)} %scan_shards.2), calls=%async_computation.1 | async-start | bytes 524288 | tf_op jit(solution)/shard_map/all_to_all | solution.py:546
  56.2 0.7 copy-start.1
  56.9 3.9 %copy-start.7 = (bf16[128,1152]{1,0:T(8,128)(2,1)S(1)}, bf16[128,1152]{1,0:T(8,128)(2,1)}, u32[]{:S(2)}) copy-start(bf16[128,1152]{1,0:T(8,128)(2,1)} %get-tuple-element.38) | copy-start | bytes 884740
  73.2 21.3 %all-to-all-start.3 = ((bf16[8,16,1024]{2,1,0:T(8,128)(2,1)}), bf16[8,16,1024]{2,1,0:T(8,128)(2,1)S(1)}, u32[]{:S(2)}, u32[]{:S(2)}) async-start(bf16[8,16,1024]{2,1,0:T(8,128)(2,1)} %scan_shards.3), calls=%async_computation.3 | async-start | bytes 524288 | tf_op jit(solution)/shard_map/all_to_all | solution.py:546
  79.7 52.0 %collective-permute-start.5 = (bf16[256,1024]{1,0:T(8,128)(2,1)}, bf16[256,1024]{1,0:T(8,128)(2,1)S(1)}, u32[]{:S(2)}, u32[]{:S(2)}) collective-permute-start(bf16[256,1024]{1,0:T(8,128)(2,1)} %outputs.10.rest_0_), channel_id=1, source_target_pairs={{0,3},{1,2},{2,1},{3,0},{4,7},{5,6},{6,5},{7,4},{8,11},{9,10},{10,... | collective-permute-start | bytes 1572872 | tf_op jit(solution)/shard_map/ppermute | solution.py:555
  87.6 44.8 %collective-permute-start.7 = (bf16[384,1024]{1,0:T(8,128)(2,1)}, bf16[384,1024]{1,0:T(8,128)(2,1)S(1)}, u32[]{:S(2)}, u32[]{:S(2)}) collective-permute-start(bf16[384,1024]{1,0:T(8,128)(2,1)} %outputs.12.rest_0_), channel_id=1, source_target_pairs={{0,2},{1,3},{2,0},{3,1},{4,6},{5,7},{6,4},{7,5},{8,10},{9,11},{10,... | collective-permute-start | bytes 2359304 | tf_op jit(solution)/shard_map/ppermute | solution.py:555
  94.1 39.1 %collective-permute-start.8 = (bf16[384,1024]{1,0:T(8,128)(2,1)}, bf16[384,1024]{1,0:T(8,128)(2,1)S(1)}, u32[]{:S(2)}, u32[]{:S(2)}) collective-permute-start(bf16[384,1024]{1,0:T(8,128)(2,1)} %outputs.17), channel_id=1, source_target_pairs={{0,1},{1,0},{2,3},{3,2},{4,5},{5,4},{6,7},{7,6},{8,9},{9,8},{10,11... | collective-permute-start | bytes 2359304 | tf_op jit(solution)/shard_map/ppermute | solution.py:555
  94.5 0.7 copy-start
  113.6 8.7 %copy-start.6 = (bf16[128,1024]{1,0:T(8,128)(2,1)S(1)}, bf16[128,1024]{1,0:T(8,128)(2,1)}, u32[]{:S(2)}) copy-start(bf16[128,1024]{1,0:T(8,128)(2,1)} %outputs.11.rest_0_) | copy-start | bytes 786436
  113.6 16.8 %copy-start.4 = (bf16[256,1024]{1,0:T(8,128)(2,1)S(1)}, bf16[256,1024]{1,0:T(8,128)(2,1)}, u32[]{:S(2)}) copy-start(bf16[256,1024]{1,0:T(8,128)(2,1)} %outputs.14.rest_0_) | copy-start | bytes 1572868
  113.6 18.1 %copy-start.3 = (bf16[256,1024]{1,0:T(8,128)(2,1)S(1)}, bf16[256,1024]{1,0:T(8,128)(2,1)}, u32[]{:S(2)}) copy-start(bf16[256,1024]{1,0:T(8,128)(2,1)} %outputs.15.rest_0_) | copy-start | bytes 1572868
  113.6 18.7 %copy-start.5 = (bf16[128,1024]{1,0:T(8,128)(2,1)S(1)}, bf16[128,1024]{1,0:T(8,128)(2,1)}, u32[]{:S(2)}) copy-start(bf16[128,1024]{1,0:T(8,128)(2,1)} %outputs.13.rest_0_) | copy-start | bytes 786436
  113.6 19.6 %copy-start.2 = (bf16[128,1024]{1,0:T(8,128)(2,1)S(1)}, bf16[128,1024]{1,0:T(8,128)(2,1)}, u32[]{:S(2)}) copy-start(bf16[128,1024]{1,0:T(8,128)(2,1)} %outputs.16.rest_0_) | copy-start | bytes 786436
  122.1 11.8 %collective-permute-start.9 = (bf16[384,1024]{1,0:T(8,128)(2,1)}, bf16[384,1024]{1,0:T(8,128)(2,1)S(1)}, u32[]{:S(2)}, u32[]{:S(2)}) collective-permute-start(bf16[384,1024]{1,0:T(8,128)(2,1)} %get-tuple-element.45), channel_id=1, source_target_pairs={{0,1},{1,0},{2,3},{3,2},{4,5},{5,4},{6,7},{7,6},{8,9},{9,8},{10,11... | collective-permute-start | bytes 2359304 | tf_op jit(solution)/shard_map/ppermute | solution.py:555
  122.3 8.1 %collective-permute-start.6 = (bf16[128,1024]{1,0:T(8,128)(2,1)S(1)}, bf16[128,1024]{1,0:T(8,128)(2,1)S(1)}, u32[]{:S(2)}, u32[]{:S(2)}) collective-permute-start(bf16[128,1024]{1,0:T(8,128)(2,1)S(1)} %copy-done.6), channel_id=1, source_target_pairs={{0,3},{1,2},{2,1},{3,0},{4,7},{5,6},{6,5},{7,4},{8,11},{9,10},{10,... | collective-permute-start | bytes 786440 | tf_op jit(solution)/shard_map/ppermute | solution.py:555
  130.4 30.6 %collective-permute-start.3 = (bf16[256,1024]{1,0:T(8,128)(2,1)S(1)}, bf16[256,1024]{1,0:T(8,128)(2,1)S(1)}, u32[]{:S(2)}, u32[]{:S(2)}) collective-permute-start(bf16[256,1024]{1,0:T(8,128)(2,1)S(1)} %copy-done.4), channel_id=1, source_target_pairs={{0,3},{1,2},{2,1},{3,0},{4,7},{5,6},{6,5},{7,4},{8,11},{9,10},{10,... | collective-permute-start | bytes 1572872 | tf_op jit(solution)/shard_map/ppermute | solution.py:555
  131.8 29.2 %collective-permute-start.4 = (bf16[256,1024]{1,0:T(8,128)(2,1)S(1)}, bf16[256,1024]{1,0:T(8,128)(2,1)S(1)}, u32[]{:S(2)}, u32[]{:S(2)}) collective-permute-start(bf16[256,1024]{1,0:T(8,128)(2,1)S(1)} %copy-done.3), channel_id=1, source_target_pairs={{0,2},{1,3},{2,0},{3,1},{4,6},{5,7},{6,4},{7,5},{8,10},{9,11},{10,... | collective-permute-start | bytes 1572872 | tf_op jit(solution)/shard_map/ppermute | solution.py:555
  132.4 28.6 %collective-permute-start.2 = (bf16[128,1024]{1,0:T(8,128)(2,1)S(1)}, bf16[128,1024]{1,0:T(8,128)(2,1)S(1)}, u32[]{:S(2)}, u32[]{:S(2)}) collective-permute-start(bf16[128,1024]{1,0:T(8,128)(2,1)S(1)} %copy-done.5), channel_id=1, source_target_pairs={{0,3},{1,2},{2,1},{3,0},{4,7},{5,6},{6,5},{7,4},{8,11},{9,10},{10,... | collective-permute-start | bytes 786440 | tf_op jit(solution)/shard_map/ppermute | solution.py:555
  133.2 33.9 %collective-permute-start.1 = (bf16[128,1024]{1,0:T(8,128)(2,1)S(1)}, bf16[128,1024]{1,0:T(8,128)(2,1)S(1)}, u32[]{:S(2)}, u32[]{:S(2)}) collective-permute-start(bf16[128,1024]{1,0:T(8,128)(2,1)S(1)} %copy-done.2), channel_id=1, source_target_pairs={{0,2},{1,3},{2,0},{3,1},{4,6},{5,7},{6,4},{7,5},{8,10},{9,11},{10,... | collective-permute-start | bytes 786440 | tf_op jit(solution)/shard_map/ppermute | solution.py:555
